TPU v7x, 32 devices: a whole 2x2x4 slice. The times are simulated.
32 devices in a mesh: dp: 16 (over z, y, x), expert: 2 (over core).
Axes of the slice: x: 2, y: 2, z: 4, core: 2. Of those that a mesh axis runs over, the one named last changes fastest.
Arguments:
- latents: bfloat16 [4096, 2048], P('dp', 'expert'), as said below
- cotangent: bfloat16 [4096, 2048], P('dp', 'expert'), may hold values from -6 to 6
- routes: int32 [4096, 2], P('dp'), may hold values from 0 to 15, all different within a row; in each aligned block of 256 rows (0 to 255, 256 to 511, ...) at most 48 rows name the same one
- router_w: float32 [2048, 16], P('expert'), may hold values from -1 to 1
- mod_shift: bfloat16 [1, 2048], P(None, 'expert'), may hold values from -3 to 3
- mod_scale: bfloat16 [1, 2048], P(None, 'expert'), may hold values from -1.5 to 2.5
- mod_gate: bfloat16 [1, 2048], P(None, 'expert'), may hold values from -4 to 4
- gate_w: bfloat16 [16, 2048, 1024], P('dp', None, 'expert'), may hold values from -0.125 to 0.125
- up_w: bfloat16 [16, 2048, 1024], P('dp', None, 'expert'), may hold values from -0.125 to 0.125
- down_w: bfloat16 [16, 1024, 2048], P('dp', 'expert'), may hold values from -0.1875 to 0.1875
Outputs:
- latent_gradient: bfloat16 [4096, 2048], P('dp', 'expert')
- grad_gate_w: bfloat16 [16, 2048, 1024], P('dp', None, 'expert')
- grad_up_w: bfloat16 [16, 2048, 1024], P('dp', None, 'expert')
- grad_down_w: bfloat16 [16, 1024, 2048], P('dp', 'expert')
- grad_router: float32 [2048, 16], P('expert')
Inputs may be any that keep to these rules, and one draw needn't show every extreme that they name: `routes`: the two experts of a token differ. Among the 256 tokens of one aligned block (the tokens of one index of dp), no expert is named more than 48 times, a bound that some block reaches. Columns and rows of latents have unlike scales.
All inputs are finite; a program needn't handle non-finite values.
Results may differ from a plain program's by a relative error of at most 0.008.
Values may be sent and summed in bfloat16 or wider, within the bound.
No kernel may reach another device: no remote copies, remote signals or barrier semaphores. Data moves between devices by JAX's collectives and lax.ppermute only.
A program may use at most 128 MiB of HBM per device.

v0:
```python
import functools

import jax
import jax.numpy as jnp
from jax import lax
from jax.experimental import pallas as pl
from jax.experimental.pallas import tpu as pltpu
from jax.sharding import PartitionSpec as P


SEQ = 4096

norm_eps = 1e-06
HIGHEST = lax.Precision.HIGHEST
F32 = jnp.float32
BF16 = jnp.bfloat16


def slot_targets(routes, experts, capacity):
    flat_routes = routes.reshape(-1)
    expert_ids = jnp.arange(experts, dtype=jnp.int32)
    onehot = (flat_routes[:, None] == expert_ids[None, :]).astype(jnp.int32)
    rank_run = jnp.cumsum(onehot, axis=0) - 1
    slots = flat_routes * capacity + jnp.sum(onehot * rank_run, axis=1)
    return slots.reshape(routes.shape)


def pair_swap(value):
    return lax.ppermute(value, "expert", [(0, 1), (1, 0)])


def core_sum(value):
    if lax.axis_size("expert") == 2:
        return value + pair_swap(value)
    return lax.psum(value, "expert")


def whole_features(part):
    if lax.axis_size("expert") == 2:
        other = pair_swap(part)
        first = lax.axis_index("expert") == 0
        return jnp.concatenate(
            [jnp.where(first, part, other), jnp.where(first, other, part)], axis=-1
        )
    return lax.all_gather(part, "expert", axis=part.ndim - 1, tiled=True)


def scatter_features(value):
    if lax.axis_size("expert") == 2:
        half = value.shape[-1] // 2
        low, high = value[..., :half], value[..., half:]
        first = lax.axis_index("expert") == 0
        other = pair_swap(jnp.where(first, high, low))
        return jnp.where(first, low, high).astype(F32) + other.astype(F32)
    return lax.psum_scatter(
        value, "expert", scatter_dimension=value.ndim - 1, tiled=True
    ).astype(F32)


def dp_sum(value):
    size = lax.axis_size("dp")
    step = 1
    while step < size:
        if size % (2 * step):
            return lax.psum(value, "dp")
        step *= 2
    step = 1
    while step < size:
        value = value + lax.ppermute(value, "dp", [(i, i ^ step) for i in range(size)])
        step *= 2
    return value


def all_to_all(value):
    return lax.all_to_all(value, "dp", split_axis=0, concat_axis=0, tiled=True)


def owner_view(arrived, groups, local):
    shaped = arrived.reshape((groups, local) + arrived.shape[1:])
    shaped = jnp.swapaxes(shaped, 0, 1)
    return shaped.reshape((local, groups * arrived.shape[1]) + arrived.shape[2:])


def sender_view(outgoing, groups):
    local = outgoing.shape[0]
    capacity = outgoing.shape[1] // groups
    shaped = outgoing.reshape((local, groups, capacity) + outgoing.shape[2:])
    shaped = jnp.swapaxes(shaped, 0, 1)
    return shaped.reshape((groups * local, capacity) + outgoing.shape[2:])


def selected_row(table, sample_index):
    return lax.dynamic_slice_in_dim(table, sample_index, 1, 0).astype(F32)


def split_bf16(value):
    high = value.astype(BF16)
    low = (value - high.astype(F32)).astype(BF16)
    return high, low


def spread_device(
    latents, cotangent, routes, router_w, mod_shift, mod_scale, mod_gate, gate_w, up_w, down_w
):
    tok_rows, width = latents.shape
    experts = router_w.shape[1]
    local = gate_w.shape[0]
    groups = lax.axis_size("dp")
    entire_width = width * lax.axis_size("expert")
    capacity = 3 * tok_rows // experts
    slot_count = experts * capacity
    sample_index = lax.axis_index("dp") * tok_rows // SEQ

    targets = slot_targets(routes, experts, capacity)
    slot_ids = jnp.arange(slot_count, dtype=jnp.int32)
    hit0 = targets[:, 0][None, :] == slot_ids[:, None]
    hit1 = targets[:, 1][None, :] == slot_ids[:, None]
    fill = (hit0 | hit1).astype(BF16)

    def to_slots(rows_b):
        rows = jnp.dot(fill, rows_b, preferred_element_type=F32).astype(BF16)
        return rows.reshape(experts, capacity, width)

    cot = cotangent.astype(F32)
    scaled_dy = (selected_row(mod_gate, sample_index) * cot).astype(BF16)
    got_z = all_to_all(to_slots(scaled_dy))

    x = latents.astype(F32)
    sums = jnp.stack([jnp.sum(x, axis=1), jnp.sum(x * x, axis=1)])
    mean, msq = core_sum(sums) / entire_width
    inv_std = lax.rsqrt(msq - mean * mean + norm_eps)[:, None]
    xhat = (x - mean[:, None]) * inv_std
    amp = 1.0 + selected_row(mod_scale, sample_index)
    normed = xhat * amp + selected_row(mod_shift, sample_index)
    got_x = all_to_all(to_slots(normed.astype(BF16)))

    logits = core_sum(lax.dot_general(
        router_w, normed, (((0,), (1,)), ((), ())), precision=HIGHEST
    )).T
    chances = jax.nn.sigmoid(logits)
    expert_ids = jnp.arange(experts, dtype=jnp.int32)
    hits = routes[:, :, None] == expert_ids[None, None, :]
    picked = jnp.sum(jnp.where(hits, chances[:, None, :], 0.0), axis=2)
    pick_sum = jnp.sum(picked, axis=1, keepdims=True)
    weights = picked / pick_sum
    w0, w1 = weights[:, 0], weights[:, 1]
    send_w = jnp.sum(
        jnp.where(hit0, w0[None, :], 0.0) + jnp.where(hit1, w1[None, :], 0.0), axis=1
    ).astype(BF16)
    got_w = all_to_all(send_w.reshape(experts, capacity))

    rows_z = owner_view(whole_features(got_z), groups, local)
    rows_x = owner_view(whole_features(got_x), groups, local)
    slot_w = owner_view(got_w, groups, local).astype(F32)[..., None]

    down_back = jnp.einsum("esd,ehd->esh", rows_z, down_w, preferred_element_type=F32)
    gate_lin = jnp.einsum("esd,edh->esh", rows_x, gate_w, preferred_element_type=F32)
    up_lin = jnp.einsum("esd,edh->esh", rows_x, up_w, preferred_element_type=F32)
    gate_sig = jax.nn.sigmoid(gate_lin)
    gate_act = gate_lin * gate_sig
    hidden = gate_act * up_lin
    slot_score = jnp.sum(hidden * down_back, axis=-1)
    d_gate = down_back * up_lin * gate_sig * (1.0 + gate_lin * (1.0 - gate_sig))
    d_up = down_back * gate_act
    part = (
        jnp.einsum("esh,edh->esd", d_gate.astype(BF16), gate_w, preferred_element_type=F32)
        + jnp.einsum("esh,edh->esd", d_up.astype(BF16), up_w, preferred_element_type=F32)
    ).astype(BF16)
    summed = scatter_features(part).astype(BF16)

    back_scores = all_to_all(sender_view(slot_score, groups)).reshape(-1)
    back_rows = all_to_all(sender_view(summed, groups)).reshape(slot_count, width)

    gate_wt = (slot_w * d_gate).astype(BF16)
    up_wt = (slot_w * d_up).astype(BF16)
    hidden_wt = (slot_w * hidden).astype(BF16)
    grad_gate = jnp.einsum("esd,esh->edh", rows_x, gate_wt, preferred_element_type=F32)
    grad_up = jnp.einsum("esd,esh->edh", rows_x, up_wt, preferred_element_type=F32)
    grad_down = jnp.einsum("esh,esd->ehd", hidden_wt, rows_z, preferred_element_type=F32)

    score_row = back_scores[:, None]
    score = core_sum(jnp.stack([
        jnp.sum(jnp.where(hit0, score_row, 0.0), axis=0),
        jnp.sum(jnp.where(hit1, score_row, 0.0), axis=0),
    ])).T
    mean_score = jnp.sum(weights * score, axis=1, keepdims=True)
    d_pick = (score - mean_score) / pick_sum * picked * (1.0 - picked)
    dlogit = jnp.sum(jnp.where(hits, d_pick[:, :, None], 0.0), axis=1)
    grad_router = dp_sum(lax.dot_general(
        dlogit, normed, (((0,), (0,)), ((), ())), precision=HIGHEST
    )).T

    mix = jnp.where(hit0, w0[None, :], 0.0) + jnp.where(hit1, w1[None, :], 0.0)
    mix_high, mix_low = split_bf16(mix)
    contract = (((0,), (0,)), ((), ()))
    combined = lax.dot_general(
        mix_high, back_rows, contract, preferred_element_type=F32
    ) + lax.dot_general(mix_low, back_rows, contract, preferred_element_type=F32)
    dnormed = combined + lax.dot_general(
        dlogit, router_w, (((1,), (1,)), ((), ())), precision=HIGHEST
    )
    dxhat = dnormed * amp
    m_one, m_two = core_sum(
        jnp.stack([jnp.sum(dxhat, axis=1), jnp.sum(dxhat * xhat, axis=1)])
    ) / entire_width
    latent_gradient = inv_std * (dxhat - m_one[:, None] - xhat * m_two[:, None]) + cot
    return (
        latent_gradient.astype(BF16),
        grad_gate.astype(BF16),
        grad_up.astype(BF16),
        grad_down.astype(BF16),
        grad_router,
    )


FEATURE_TILE = 512


def after(value, *deps):
    return lax.optimization_barrier((value,) + deps)[0]


def dp_total(value):
    size = lax.axis_size("dp")
    if size % 4:
        return dp_sum(value)
    step = 1
    while step < size:
        far = 3 if step * 2 < size else 1
        others = []
        for k in range(1, far + 1):
            others.append(
                lax.ppermute(value, "dp", [(i, i ^ (step * k)) for i in range(size)])
            )
        value = value + others[0]
        if far == 3:
            value = value + (others[1] + others[2])
        step *= far + 1
    return value


def dp_exchange(value):
    size = lax.axis_size("dp")
    index = lax.axis_index("dp")
    step = 1
    while step < size:
        clear = (index & step) == 0
        pairs = value.reshape(size // 2, 2, -1)
        low, high = pairs[:, 0], pairs[:, 1]
        kept, sent = jnp.where(clear, low, high), jnp.where(clear, high, low)
        other = lax.ppermute(sent, "dp", [(i, i ^ step) for i in range(size)])
        value = jnp.concatenate([jnp.where(clear, kept, other), jnp.where(clear, other, kept)])
        step *= 2
    return value


def lin(rows, weight):
    return jnp.dot(rows, weight, preferred_element_type=F32)


def lin_t(rows, weight):
    return lax.dot_general(rows, weight, (((1,), (1,)), ((), ())), preferred_element_type=F32)


def lin_rows(left, right):
    return lax.dot_general(left, right, (((0,), (0,)), ((), ())), preferred_element_type=F32)


def expert_body(
    core, own, oth, slot_w, coefs, router_own, router_oth, down_hbm, gate_hbm, up_hbm,
    part_own, part_oth, gate_wt, up_wt, hidden_wt, high, low,
    x_s, z_s, down_s, gate_s, up_s, own_s, oth_s, wt_s, row_sems, sems, out_sems,
):
    groups, chunk, width = x_s.shape[1:]
    rows = groups * chunk

    def start(source, target, sem):
        copy = pltpu.make_async_copy(source, target, sem)
        copy.start()
        return copy

    def arrived(kind, scratch):
        return [
            start(ref.at[:, pl.ds(kind * chunk, chunk)], scratch.at[place], row_sems.at[kind, place])
            for place, ref in enumerate((own, oth))
        ]

    def halves(index, hbm, scratch):
        copies = []
        for place in range(2):
            first = pl.multiple_of(((core[0] + place) % 2) * width, width)
            source = hbm.at[:, pl.ds(first, width)] if index == 0 else hbm.at[pl.ds(first, width)]
            copies.append(start(source, scratch.at[place], sems.at[index, place]))
        return copies

    z_copies, down_copies = arrived(1, z_s), halves(0, down_hbm, down_s)
    x_copies, gate_copies = arrived(0, x_s), halves(1, gate_hbm, gate_s)
    up_copies = halves(2, up_hbm, up_s)

    def rows_of(scratch, place):
        return scratch[place].reshape(rows, width)

    def total(product, scratch, copies, weight, weight_copies):
        parts = []
        for place in range(2):
            for copy in (copies[place], weight_copies[place]):
                if copy is not None:
                    copy.wait()
            parts.append(product(rows_of(scratch, place), weight[place]))
        return parts[0] + parts[1]

    down_back = total(lin_t, z_s, z_copies, down_s, down_copies)
    gate_lin = total(lin, x_s, x_copies, gate_s, gate_copies)
    gate_sig = jax.nn.sigmoid(gate_lin)
    up_lin = total(lin, x_s, (None, None), up_s, up_copies)
    gate_act = gate_lin * gate_sig
    hidden = gate_act * up_lin
    scored = jnp.sum(hidden * down_back, axis=1, keepdims=True) * coefs[...]
    scored_b = scored.astype(BF16)
    high[...] = scored_b
    low[...] = (scored - scored_b.astype(F32)).astype(BF16)
    back = slot_w[...] * down_back
    wt_s[0] = (back * up_lin * gate_sig * (1.0 + gate_lin * (1.0 - gate_sig))).astype(BF16)
    wt_s[1] = (back * gate_act).astype(BF16)
    saves = []
    for place, router, scratch, out in ((1, router_oth, oth_s, part_oth), (0, router_own, own_s, part_own)):
        scratch[...] = (
            lin_t(wt_s[0], gate_s[place]) + lin_t(wt_s[1], up_s[place]) + lin(scored_b, router[...])
        ).astype(BF16)
        saves.append(start(scratch, out, out_sems.at[3 + place]))
        if place == 1:
            wt_s[2] = (slot_w[...] * hidden).astype(BF16)
            for k, ref in enumerate((gate_wt, up_wt, hidden_wt)):
                saves.append(start(wt_s.at[k], ref, out_sems.at[k]))
    for copy in saves:
        copy.wait()


def expert_rows(core, own, oth, slot_w, coefs, router_own, router_oth, down_w, gate_w, up_w):
    groups, span, width = own.shape
    chunk = span // 2
    rows = groups * chunk
    hidden = gate_w.shape[1]
    wide = jax.ShapeDtypeStruct((rows, width), BF16)
    deep = jax.ShapeDtypeStruct((rows, hidden), BF16)
    narrow = jax.ShapeDtypeStruct(coefs.shape, BF16)
    whole = pl.BlockSpec(memory_space=pltpu.VMEM)
    raw = pl.BlockSpec(memory_space=pl.ANY)
    return pl.pallas_call(
        expert_body,
        name="expert_rows",
        in_specs=[pl.BlockSpec(memory_space=pltpu.SMEM)] + [raw] * 2 + [whole] * 4 + [raw] * 3,
        out_specs=[raw] * 5 + [whole] * 2,
        scratch_shapes=[
            pltpu.VMEM((2, groups, chunk, width), BF16),
            pltpu.VMEM((2, groups, chunk, width), BF16),
            pltpu.VMEM((2, hidden, width), BF16),
            pltpu.VMEM((2, width, hidden), BF16),
            pltpu.VMEM((2, width, hidden), BF16),
            pltpu.VMEM((rows, width), BF16),
            pltpu.VMEM((rows, width), BF16),
            pltpu.VMEM((3, rows, hidden), BF16),
            pltpu.SemaphoreType.DMA((2, 2)),
            pltpu.SemaphoreType.DMA((3, 2)),
            pltpu.SemaphoreType.DMA((5,)),
        ],
        out_shape=[wide, wide, deep, deep, deep, narrow, narrow],
        cost_estimate=pl.CostEstimate(
            flops=20 * rows * width * hidden,
            bytes_accessed=12 * width * hidden + 12 * rows * width + 6 * rows * hidden,
            transcendentals=rows * hidden,
        ),
    )(core, own, oth, slot_w, coefs, router_own, router_oth, down_w, gate_w, up_w)


def flat(ref):
    groups, chunk, width = ref.shape
    return ref[...].reshape(groups * chunk, width)


def router_body(own_1, oth_1, own_2, oth_2, high_1, low_1, high_2, low_2, own, oth):
    for one, two, out in ((own_1, own_2, own), (oth_1, oth_2, oth)):
        x_1, x_2 = flat(one), flat(two)
        out[...] = (
            lin_rows(high_1[...], x_1) + lin_rows(low_1[...], x_1)
            + lin_rows(high_2[...], x_2) + lin_rows(low_2[...], x_2)
        )


def router_grads(own_1, oth_1, own_2, oth_2, *scores):
    groups, _, width = own_1.shape
    experts = scores[0].shape[1]
    rows = scores[0].shape[0] + scores[2].shape[0]
    tile = FEATURE_TILE if width % FEATURE_TILE == 0 else width
    out = jax.ShapeDtypeStruct((experts, width), F32)
    blocks = [
        pl.BlockSpec((groups, ref.shape[1] // 2, tile), lambda i: (0, 0, i))
        for ref in (own_1, oth_1, own_2, oth_2)
    ]
    full = [pl.BlockSpec(score.shape, lambda i: (0, 0)) for score in scores]
    return pl.pallas_call(
        router_body,
        name="router_grads",
        grid=(width // tile,),
        in_specs=blocks + full,
        out_specs=[pl.BlockSpec((experts, tile), lambda i: (0, i))] * 2,
        out_shape=[out, out],
        cost_estimate=pl.CostEstimate(
            flops=8 * rows * width * experts,
            bytes_accessed=4 * rows * width,
            transcendentals=0,
        ),
    )(own_1, oth_1, own_2, oth_2, *scores)


def weight_body(
    core, x_1, z_1, x_2, z_2, gate_1, up_1, hidden_1, gate_2, up_2, hidden_2, *refs
):
    grad_gate, grad_up, grad_down = refs[-3:]
    first, second = flat(x_1), flat(x_2)
    grad_gate[...] = (lin_rows(first, gate_1[...]) + lin_rows(second, gate_2[...])).astype(BF16)
    grad_up[...] = (lin_rows(first, up_1[...]) + lin_rows(second, up_2[...])).astype(BF16)
    grad_down[...] = (
        lin_rows(hidden_1[...], flat(z_1)) + lin_rows(hidden_2[...], flat(z_2))
    ).astype(BF16)


def weight_grads(core, place, part_1, part_2, weighted, begun=()):
    groups, _, width = part_1.shape
    hidden = weighted[0].shape[1]
    rows = weighted[0].shape[0] + weighted[3].shape[0]
    tile = FEATURE_TILE if width % FEATURE_TILE == 0 else width
    steps = width // tile

    def block(ref, kind):
        return pl.BlockSpec(
            (groups, ref.shape[1] // 2, tile), lambda i, core: (0, kind, i)
        )

    blocks = [block(ref, kind) for ref in (part_1, part_2) for kind in range(2)]
    full = [pl.BlockSpec(value.shape, lambda i, core: (0, 0)) for value in weighted]
    raw = [pl.BlockSpec(memory_space=pl.ANY)] * len(begun)
    by_rows = pl.BlockSpec((tile, hidden), lambda i, core: (((core[0] + place) % 2) * steps + i, 0))
    by_columns = pl.BlockSpec((hidden, tile), lambda i, core: (0, ((core[0] + place) % 2) * steps + i))
    tall = jax.ShapeDtypeStruct((2 * width, hidden), BF16)
    return pl.pallas_call(
        weight_body,
        name="weight_grads",
        grid_spec=pltpu.PrefetchScalarGridSpec(
            num_scalar_prefetch=1,
            grid=(steps,),
            in_specs=blocks + full + raw,
            out_specs=[by_rows, by_rows, by_columns],
        ),
        out_shape=[tall, tall, jax.ShapeDtypeStruct((hidden, 2 * width), BF16)],
        input_output_aliases={11 + k: k for k in range(len(begun))},
        cost_estimate=pl.CostEstimate(
            flops=6 * rows * width * hidden,
            bytes_accessed=6 * width * hidden + 4 * rows * width + 6 * rows * hidden,
            transcendentals=0,
        ),
    )(core, part_1, part_1, part_2, part_2, *weighted, *begun)


FILL_BYTES = 24 * 2**20


def fill_body(first, targets, x_rows, z_rows, out):
    experts, span, width = out.shape
    chunk = span // 2
    capacity = 3 * targets.shape[1] // experts
    rows = experts * chunk
    index = lax.broadcasted_iota(jnp.int32, (rows, targets.shape[1]), 0)
    ids = (index // chunk * capacity + index % chunk + first).astype(F32)
    hit = (targets[0:1, :] == ids) | (targets[1:2, :] == ids)
    fill = jnp.where(hit, 1.0, 0.0).astype(BF16)
    out[:, :chunk, :] = lin(fill, x_rows[...]).astype(BF16).reshape(experts, chunk, width)
    out[:, chunk:, :] = lin(fill, z_rows[...]).astype(BF16).reshape(experts, chunk, width)


def fill_slots(targets, x_rows, z_rows, experts, first, chunk):
    width = x_rows.shape[1]
    return pl.pallas_call(
        functools.partial(fill_body, first),
        name="fill_slots",
        compiler_params=pltpu.CompilerParams(vmem_limit_bytes=FILL_BYTES),
        out_shape=jax.ShapeDtypeStruct((experts, 2 * chunk, width), BF16),
    )(targets, x_rows, z_rows)


def per_device(
    latents, cotangent, routes, router_w, mod_shift, mod_scale, mod_gate, gate_w, up_w, down_w
):
    size = lax.axis_size("dp")
    if lax.axis_size("expert") != 2 or size & (size - 1) or gate_w.shape[0] != 1 or latents.shape[0] % 256:
        return spread_device(
            latents, cotangent, routes, router_w, mod_shift, mod_scale, mod_gate,
            gate_w, up_w, down_w,
        )
    tok_rows, width = latents.shape
    experts = router_w.shape[1]
    entire_width = 2 * width
    capacity = 3 * tok_rows // experts
    slot_count = experts * capacity
    dp_index = lax.axis_index("dp")
    sample_index = dp_index * tok_rows // SEQ
    core = lax.axis_index("expert").astype(jnp.int32).reshape(1)
    gate_w, up_w, down_w = gate_w[0], up_w[0], down_w[0]

    expert_ids = lax.broadcasted_iota(jnp.int32, (experts, tok_rows), 0)
    named = [routes[:, k][None, :] == expert_ids for k in range(2)]
    named_b = (named[0] | named[1]).astype(BF16)
    rows_i = lax.broadcasted_iota(jnp.int32, (tok_rows, tok_rows), 0)
    cols_i = lax.broadcasted_iota(jnp.int32, (tok_rows, tok_rows), 1)
    places = lin(named_b, (rows_i < cols_i).astype(BF16)) + (expert_ids * capacity).astype(F32)
    targets = [jnp.sum(jnp.where(n, places, 0.0), axis=0) for n in named]
    first = capacity // 3 * 2
    parts = ((0, first), (first, capacity - first))

    def slot_of(index, first, length):
        return (index // length * capacity + index % length + first).astype(F32)

    cot = cotangent.astype(F32)
    scaled_dy = (selected_row(mod_gate, sample_index) * cot).astype(BF16)
    x = latents.astype(F32)
    sums = jnp.stack([jnp.sum(x, axis=1), jnp.sum(x * x, axis=1)])
    mean, msq = core_sum(sums) / entire_width
    inv_std = lax.rsqrt(msq - mean * mean + norm_eps)[:, None]
    xhat = (x - mean[:, None]) * inv_std
    amp = 1.0 + selected_row(mod_scale, sample_index)
    normed = xhat * amp + selected_row(mod_shift, sample_index)
    normed_b = normed.astype(BF16)
    second = capacity - first
    send_1 = fill_slots(jnp.stack(targets), normed_b, scaled_dy, experts, 0, first)
    send_2 = fill_slots(
        after(jnp.stack(targets), send_1), normed_b, scaled_dy, experts, first, second
    )
    own_1 = all_to_all(send_1)
    own_2 = all_to_all(send_2)

    logits = core_sum(lax.dot_general(
        router_w, after(normed, send_1), (((0,), (1,)), ((), ())), precision=HIGHEST
    ))
    chances = jax.nn.sigmoid(logits)
    picked = jnp.stack([jnp.sum(jnp.where(n, chances, 0.0), axis=0) for n in named])
    pick_sum = jnp.sum(picked, axis=0, keepdims=True)
    weights = picked / pick_sum
    slopes = weights[::-1] * picked * (1.0 - picked) / pick_sum
    other_ids = routes.T[::-1].astype(F32)
    slot_row = lax.broadcasted_iota(jnp.int32, (tok_rows, slot_count), 1).astype(F32)
    hits = [t[:, None] == slot_row for t in targets]

    def of_slots(pair):
        return jnp.sum(
            jnp.where(hits[0], pair[0][:, None], 0.0) + jnp.where(hits[1], pair[1][:, None], 0.0),
            axis=0,
        ).reshape(experts, capacity)

    kinds = (weights, slopes, slopes[::-1], other_ids)
    sent = jnp.concatenate([of_slots(pair) for pair in kinds], axis=1)
    arrived = dp_exchange(sent)
    columns = []
    for start, length in parts:
        rows = experts * length
        ids = lax.broadcasted_iota(jnp.int32, (rows, experts), 1).astype(F32)
        slot_w, slope, slope_other, other = [
            arrived[:, k * capacity + start:k * capacity + start + length].reshape(rows, 1)
            for k in range(4)
        ]
        coefs = jnp.where(ids == dp_index.astype(F32), slope, 0.0) - jnp.where(
            ids == other, slope_other, 0.0
        )
        columns.append((slot_w, coefs))
    router_own = router_w.T.astype(BF16)
    router_oth = pair_swap(after(router_own, send_1))
    joins = []
    for start, length in parts:
        ids = slot_of(
            lax.broadcasted_iota(jnp.int32, (tok_rows, experts * length), 1), start, length
        )
        joins.append(((targets[0][:, None] == ids) | (targets[1][:, None] == ids)).astype(BF16))

    oth_1 = pair_swap(own_1)
    part_own, part_oth, gate_1, up_1, hidden_1, high_1, low_1 = expert_rows(
        core, own_1, oth_1, *columns[0], router_own, router_oth, down_w, gate_w, up_w
    )
    back_1 = (part_own.astype(F32) + pair_swap(part_oth).astype(F32)).astype(BF16)
    back_1 = all_to_all(after(back_1, own_2).reshape(experts, first, width))
    oth_2 = pair_swap(own_2)
    part_own, part_oth, gate_2, up_2, hidden_2, high_2, low_2 = expert_rows(
        core, own_2, oth_2, *columns[1], router_own, router_oth, down_w, gate_w, up_w
    )
    back_2 = (part_own.astype(F32) + pair_swap(part_oth).astype(F32)).astype(BF16)
    weighted = (gate_1, up_1, hidden_1, gate_2, up_2, hidden_2)
    begun = weight_grads(core, 0, after(own_1, back_2), own_2, weighted)
    back_2 = all_to_all(after(back_2, back_1).reshape(experts, second, width))

    router_own, router_oth = router_grads(own_1, oth_1, own_2, oth_2, high_1, low_1, high_2, low_2)
    grad_gate, grad_up, grad_down = weight_grads(
        core, 1, oth_1, oth_2, weighted, begun
    )
    grad_router = dp_total(router_own + pair_swap(router_oth)).T

    combined = lin(joins[0], back_1.reshape(-1, width))
    dxhat = (combined + lin(joins[1], back_2.reshape(-1, width))) * amp
    m_one, m_two = core_sum(
        jnp.stack([jnp.sum(dxhat, axis=1), jnp.sum(dxhat * xhat, axis=1)])
    ) / entire_width
    latent_gradient = inv_std * (dxhat - m_one[:, None] - xhat * m_two[:, None]) + cot
    return (
        latent_gradient.astype(BF16), grad_gate[None], grad_up[None], grad_down[None], grad_router
    )


def solution(mesh):
    placed = (
        P("dp", "expert"),
        P("dp", "expert"),
        P("dp", None),
        P("expert", None),
        P(None, "expert"),
        P(None, "expert"),
        P(None, "expert"),
        P("dp", None, "expert"),
        P("dp", None, "expert"),
        P("dp", "expert", None),
    )
    return jax.shard_map(
        per_device,
        mesh=mesh,
        in_specs=placed,
        out_specs=(
            P("dp", "expert"),
            P("dp", None, "expert"),
            P("dp", None, "expert"),
            P("dp", "expert", None),
            P("expert", None),
        ),
        check_vma=False,
    )
```

profile of v0, /device:TPU:0, one launch (start us, length us, event | category | flops | bytes accessed | tf_op | source)
XLA Modules:
  0.0 172.6 jit_solution(13038592482363077862)
XLA Ops:
  0.6 1.3 convert_reduce_fusion
  1.9 0.6 collective-permute-start
  2.5 0.8 fusion.81
  3.3 0.7 convert_add_fusion.1
  3.9 0.1 select_reduce_fusion.3
  4.1 0.7 add.167
  4.8 0.7 mul.121
  5.6 1.6 fusion.8
  7.1 2.0 %fill_slots.2 = bf16[16,64,1024]{2,1,0:T(8,128)(2,1)} custom-call(f32[2,256]{1,0:T(2,128)S(1)} %pad_maximum_fusion.6.targets, bf16[256,1024]{1,0:T(8,128)(2,1)S(1)} %get-tuple-element.74.x_rows, bf16[256,1024]{1,0:T(8,128)(2,1)S(1)} %get-tuple-element.116.z_rows), custom_call_target="tpu_custom_call" | custom-call | tf_op jit(solution)/shard_map/fill_slots/pallas_call | solution.py:483
  9.2 8.1 %all-to-all-start = ((bf16[16,64,1024]{2,1,0:T(8,128)(2,1)}), bf16[16,64,1024]{2,1,0:T(8,128)(2,1)}, u32[]{:S(2)}, u32[]{:S(2)}) async-start(bf16[16,64,1024]{2,1,0:T(8,128)(2,1)} %fill_slots.2), calls=%async_computation | async-start | bytes 4194304 | tf_op jit(solution)/shard_map/all_to_all | solution.py:75
  17.3 0.1 rev.8
  17.4 0.9 convolution_bitcast_fusion
  18.3 0.2 collective-permute-start.2
  18.5 1.0 collective-permute-done.2
  19.6 0.1 rev.7
  19.7 0.6 fusion.15
  20.3 0.1 concatenate.25
  20.4 0.1 concatenate.26
  20.4 0.1 concatenate.24
  20.5 0.1 concatenate.27
  20.6 0.1 pad_maximum_fusion
  20.8 1.9 %collective-permute-start.3 = (f32[8,192]{1,0:T(8,128)S(1)}, f32[8,192]{1,0:T(8,128)S(1)}, u32[]{:S(2)}, u32[]{:S(2)}) collective-permute-start(f32[8,192]{1,0:T(8,128)S(1)} %bitcast.107), channel_id=1, source_target_pairs={{0,2},{2,0},{4,6},{6,4},{8,10},{10,8},{12,14},{14,12},{16,18},{18,... | collective-permute-start | bytes 18440 | tf_op jit(solution)/shard_map/ppermute | solution.py:251
  22.7 3.3 %collective-permute-done.3 = f32[8,192]{1,0:T(8,128)S(1)} collective-permute-done((f32[8,192]{1,0:T(8,128)S(1)}, f32[8,192]{1,0:T(8,128)S(1)}, u32[]{:S(2)}, u32[]{:S(2)}) %collective-permute-start.3) | collective-permute-done | bytes 6176 | tf_op jit(solution)/shard_map/ppermute | solution.py:251
  26.0 2.9 %collective-permute-start.4 = (f32[8,192]{1,0:T(8,128)S(1)}, f32[8,192]{1,0:T(8,128)S(1)}, u32[]{:S(2)}, u32[]{:S(2)}) collective-permute-start(f32[8,192]{1,0:T(8,128)S(1)} %bitcast.105), channel_id=1, source_target_pairs={{0,4},{2,6},{4,0},{6,2},{8,12},{10,14},{12,8},{14,10},{16,20},{18,... | collective-permute-start | bytes 18440 | tf_op jit(solution)/shard_map/ppermute | solution.py:251
  29.0 31.5 %all-to-all-done.own.x_1.z_1.own_1 = bf16[16,64,1024]{2,1,0:T(8,128)(2,1)} async-done(((bf16[16,64,1024]{2,1,0:T(8,128)(2,1)}), bf16[16,64,1024]{2,1,0:T(8,128)(2,1)}, u32[]{:S(2)}, u32[]{:S(2)}) %all-to-all-start) | async-done | bytes 2097184 | tf_op jit(solution)/shard_map/all_to_all | solution.py:75
  60.6 6.2 %collective-permute-start.5 = (f32[8,192]{1,0:T(8,128)S(1)}, f32[8,192]{1,0:T(8,128)S(1)}, u32[]{:S(2)}, u32[]{:S(2)}) collective-permute-start(f32[8,192]{1,0:T(8,128)S(1)} %bitcast.106), channel_id=1, source_target_pairs={{0,8},{2,10},{4,12},{6,14},{8,0},{10,2},{12,4},{14,6},{16,24},{18,... | collective-permute-start | bytes 18440 | tf_op jit(solution)/shard_map/ppermute | solution.py:251
  66.8 1.6 collective-permute-done.5
  68.5 4.3 %collective-permute-start.6 = (f32[8,192]{1,0:T(8,128)S(1)}, f32[8,192]{1,0:T(8,128)S(1)}, u32[]{:S(2)}, u32[]{:S(2)}) collective-permute-start(f32[8,192]{1,0:T(8,128)S(1)} %bitcast.104), channel_id=1, source_target_pairs={{0,16},{2,18},{4,20},{6,22},{8,24},{10,26},{12,28},{14,30},{16,0},... | collective-permute-start | bytes 18440 | tf_op jit(solution)/shard_map/ppermute | solution.py:251
  72.8 1.4 fill_slots.3
  74.2 4.8 %all-to-all-start.1 = ((bf16[16,32,1024]{2,1,0:T(8,128)(2,1)}), bf16[16,32,1024]{2,1,0:T(8,128)(2,1)}, u32[]{:S(2)}, u32[]{:S(2)}) async-start(bf16[16,32,1024]{2,1,0:T(8,128)(2,1)} %fill_slots.3), calls=%async_computation.1 | async-start | bytes 2097152 | tf_op jit(solution)/shard_map/all_to_all | solution.py:75
  79.5 1.0 select_subtract_fusion.coefs
  80.4 1.0 reshape.129.slot_w
  81.4 0.6 copy-done.8
  82.0 0.7 copy-done
  82.7 12.6 %expert_rows.2 = (bf16[512,1024]{1,0:T(8,128)(2,1)}, bf16[512,1024]{1,0:T(8,128)(2,1)}, bf16[512,512]{1,0:T(8,128)(2,1)}, bf16[512,512]{1,0:T(8,128)(2,1)}, bf16...) custom-call(s32[1]{0:T(128)} %bitcast.6.core, ...), custom_call_target="tpu_custom_call" | custom-call | flops 5368709120 | bytes 14155776 | tf_op jit(solution)/shard_map/expert_rows/pallas_call | solution.py:349
  95.4 0.6 collective-permute-start.8
  95.9 6.8 %all-to-all-done.1.own.x_2.z_2.own_2 = bf16[16,32,1024]{2,1,0:T(8,128)(2,1)} async-done(((bf16[16,32,1024]{2,1,0:T(8,128)(2,1)}), bf16[16,32,1024]{2,1,0:T(8,128)(2,1)}, u32[]{:S(2)}, u32[]{:S(2)}) %all-to-all-start.1) | async-done | bytes 1048608 | tf_op jit(solution)/shard_map/all_to_all | solution.py:75
  102.7 2.6 %add_convert_fusion = bf16[512,1024]{1,0:T(8,128)(2,1)} fusion(bf16[512,1024]{1,0:T(8,128)(2,1)S(1)} %collective-permute-done.8, bf16[512,1024]{1,0:T(8,128)(2,1)} %get-tuple-element.35), kind=kLoop, calls=%fused_computation | loop fusion | flops 2097152 | bytes 3145728 | tf_op jit(solution)/shard_map/convert_element_type | solution.py:587
  105.3 5.9 %all-to-all-start.2 = ((bf16[16,32,1024]{2,1,0:T(8,128)(2,1)}), bf16[16,32,1024]{2,1,0:T(8,128)(2,1)S(1)}, u32[]{:S(2)}, u32[]{:S(2)}) async-start(bf16[16,32,1024]{2,1,0:T(8,128)(2,1)} %bitcast.30), calls=%async_computation.2 | async-start | bytes 2097152 | tf_op jit(solution)/shard_map/all_to_all | solution.py:75
  111.3 0.1 eq.141
  111.4 0.1 broadcast_in_dim.149
  111.5 0.8 reshape.130.slot_w
  112.3 0.8 select_subtract_fusion.1.coefs
  113.1 1.0 copy-done.1
  114.1 8.7 %expert_rows.3 = (bf16[256,1024]{1,0:T(8,128)(2,1)}, bf16[256,1024]{1,0:T(8,128)(2,1)}, bf16[256,512]{1,0:T(8,128)(2,1)}, bf16[256,512]{1,0:T(8,128)(2,1)}, bf16...) custom-call(s32[1]{0:T(128)} %bitcast.6.core, ...), custom_call_target="tpu_custom_call" | custom-call | flops 2684354560 | bytes 10223616 | tf_op jit(solution)/shard_map/expert_rows/pallas_call | solution.py:349
  122.8 0.3 collective-permute-start.10
  123.1 1.9 %collective-permute-done.10 = bf16[256,1024]{1,0:T(8,128)(2,1)S(1)} collective-permute-done((bf16[256,1024]{1,0:T(8,128)(2,1)}, bf16[256,1024]{1,0:T(8,128)(2,1)S(1)}, u32[]{:S(2)}, u32[]{:S(2)}) %collective-permute-start.10) | collective-permute-done | bytes 524320 | tf_op jit(solution)/shard_map/ppermute | solution.py:29
  125.0 2.0 %add_convert_fusion.1 = bf16[256,1024]{1,0:T(8,128)(2,1)} fusion(bf16[256,1024]{1,0:T(8,128)(2,1)S(1)} %collective-permute-done.10, bf16[256,1024]{1,0:T(8,128)(2,1)} %get-tuple-element.39), kind=kLoop, calls=%fused_computation.29 | loop fusion | flops 1048576 | bytes 1572864 | tf_op jit(solution)/shard_map/convert_element_type | solution.py:593
  127.0 9.1 %all-to-all-done.2 = bf16[16,32,1024]{2,1,0:T(8,128)(2,1)S(1)} async-done(((bf16[16,32,1024]{2,1,0:T(8,128)(2,1)}), bf16[16,32,1024]{2,1,0:T(8,128)(2,1)S(1)}, u32[]{:S(2)}, u32[]{:S(2)}) %all-to-all-start.2) | async-done | bytes 1048608 | tf_op jit(solution)/shard_map/all_to_all | solution.py:75
  136.0 6.8 %all-to-all-start.3 = ((bf16[16,16,1024]{2,1,0:T(8,128)(2,1)}), bf16[16,16,1024]{2,1,0:T(8,128)(2,1)S(1)}, u32[]{:S(2)}, u32[]{:S(2)}) async-start(bf16[16,16,1024]{2,1,0:T(8,128)(2,1)} %bitcast.32), calls=%async_computation.3 | async-start | bytes 1048576 | tf_op jit(solution)/shard_map/all_to_all | solution.py:75
  142.9 3.2 %router_grads.1 = (f32[16,1024]{1,0:T(8,128)}, f32[16,1024]{1,0:T(8,128)}) custom-call(bf16[16,64,1024]{2,1,0:T(8,128)(2,1)} %all-to-all-done.own.x_1.z_1.own_1, bf16[16,64,1024]{2,1,0:T(8,128)(2,1)} %copy-done, bf16[16,32,1024]{2,1,0:T(8,128)(2,1)} %all-to-all-done.1.own.x_2.z_2.own_2, bf16[16,32,1024]{2,1,0:T(8,128)(2,1)} %copy-done.1, ...), custom_call_target="tpu_custom_call" | custom-call | flops 100663296 | bytes 3145728 | tf_op jit(solution)/shard_map/router_grads/pallas_call | solution.py:401
  146.1 5.8 %weight_grads.2 = (bf16[2048,512]{1,0:T(8,128)(2,1)}, bf16[2048,512]{1,0:T(8,128)(2,1)}, bf16[512,2048]{1,0:T(8,128)(2,1)}) custom-call(s32[1]{0:T(128)} %bitcast.6.core, bf16[16,64,1024]{2,1,0:T(8,128)(2,1)} %all-to-all-done.own.x_1.z_1.own_1, bf16[16,64,1024]{2,1,0:T(8,128)(2,1)} %all-to-all-done.own.x_1.z_1.own_1, ...), custom_call_target="tpu_custom_call" | custom-call | flops 2415919104 | bytes 8650752 | tf_op jit(solution)/shard_map/weight_grads/pallas_call | solution.py:446
  151.9 2.9 %collective-permute-start.15 = (f32[16,1024]{1,0:T(8,128)S(1)}, f32[16,1024]{1,0:T(8,128)S(1)}, u32[]{:S(2)}, u32[]{:S(2)}) collective-permute-start(f32[16,1024]{1,0:T(8,128)S(1)} %add.160), channel_id=1, source_target_pairs={{0,6},{2,4},{4,2},{6,0},{8,14},{10,12},{12,10},{14,8},{16,22},{18,... | collective-permute-start | bytes 196616 | tf_op jit(solution)/shard_map/ppermute | solution.py:233
  154.8 0.6 collective-permute-start.14
  155.4 0.1 collective-permute-start.13
  155.5 5.9 %weight_grads.3 = (bf16[2048,512]{1,0:T(8,128)(2,1)}, bf16[2048,512]{1,0:T(8,128)(2,1)}, bf16[512,2048]{1,0:T(8,128)(2,1)}) custom-call(s32[1]{0:T(128)} %bitcast.6.core, bf16[16,64,1024]{2,1,0:T(8,128)(2,1)} %copy-done, bf16[16,64,1024]{2,1,0:T(8,128)(2,1)} %copy-done, ...), custom_call_target="tpu_custom_call", output_to_operand_aliasing={{0}: (11, {}), {1}: (12, {}), {2}: (13, {})} | custom-call | flops 2415919104 | bytes 8650752 | tf_op jit(solution)/shard_map/weight_grads/pallas_call | solution.py:446
  161.4 3.8 %collective-permute-start.18 = (f32[16,1024]{1,0:T(8,128)S(1)}, f32[16,1024]{1,0:T(8,128)S(1)}, u32[]{:S(2)}, u32[]{:S(2)}) collective-permute-start(f32[16,1024]{1,0:T(8,128)S(1)} %add_add_fusion.1), channel_id=1, source_target_pairs={{0,24},{2,26},{4,28},{6,30},{8,16},{10,18},{12,20},{14,22},{16,8},... | collective-permute-start | bytes 196616 | tf_op jit(solution)/shard_map/ppermute | solution.py:233
  165.2 0.7 collective-permute-start.16
  165.8 0.4 fusion.30
  166.2 0.7 fusion.71
  167.0 0.9 collective-permute-done.18
  167.9 2.8 %collective-permute-done.17 = f32[16,1024]{1,0:T(8,128)S(1)} collective-permute-done((f32[16,1024]{1,0:T(8,128)S(1)}, f32[16,1024]{1,0:T(8,128)S(1)}, u32[]{:S(2)}, u32[]{:S(2)}) %collective-permute-start.17) | collective-permute-done | bytes 65568 | tf_op jit(solution)/shard_map/ppermute | solution.py:233
  170.7 0.6 add_bitcast_fusion
  171.3 1.2 fusion.2
  (88 shorter events, 1.1 us)
Async XLA Ops:
  1.9 3.6 %collective-permute-start = (f32[2,256]{1,0:T(2,128)S(1)}, f32[2,256]{1,0:T(2,128)S(1)}, u32[]{:S(2)}, u32[]{:S(2)}) collective-permute-start(f32[2,256]{1,0:T(2,128)S(1)} %pad_maximum_fusion.5), channel_id=1, source_target_pairs={{0,1},{1,0},{2,3},{3,2},{4,5},{5,4},{6,7},{7,6},{8,9},{9,8},{10,11... | collective-permute-start | bytes 6152 | tf_op jit(solution)/shard_map/ppermute | solution.py:29
  9.2 8.1 %copy-start.7 = (s32[256,2]{0,1:T(2,128)S(1)}, s32[256,2]{0,1:T(2,128)}, u32[]{:S(2)}) copy-start(s32[256,2]{0,1:T(2,128)} %param.12) | copy-start | bytes 6148
  9.2 8.2 %copy-start.4 = (f32[1024,16]{0,1:T(8,128)S(1)}, f32[1024,16]{0,1:T(8,128)}, u32[]{:S(2)}) copy-start(f32[1024,16]{0,1:T(8,128)} %param.13) | copy-start | bytes 196612
  9.2 51.3 %all-to-all-start = ((bf16[16,64,1024]{2,1,0:T(8,128)(2,1)}), bf16[16,64,1024]{2,1,0:T(8,128)(2,1)}, u32[]{:S(2)}, u32[]{:S(2)}) async-start(bf16[16,64,1024]{2,1,0:T(8,128)(2,1)} %fill_slots.2), calls=%async_computation | async-start | bytes 4194304 | tf_op jit(solution)/shard_map/all_to_all | solution.py:75
  18.3 1.2 collective-permute-start.2
  20.8 5.2 %collective-permute-start.3 = (f32[8,192]{1,0:T(8,128)S(1)}, f32[8,192]{1,0:T(8,128)S(1)}, u32[]{:S(2)}, u32[]{:S(2)}) collective-permute-start(f32[8,192]{1,0:T(8,128)S(1)} %bitcast.107), channel_id=1, source_target_pairs={{0,2},{2,0},{4,6},{6,4},{8,10},{10,8},{12,14},{14,12},{16,18},{18,... | collective-permute-start | bytes 18440 | tf_op jit(solution)/shard_map/ppermute | solution.py:251
  26.0 34.5 %collective-permute-start.4 = (f32[8,192]{1,0:T(8,128)S(1)}, f32[8,192]{1,0:T(8,128)S(1)}, u32[]{:S(2)}, u32[]{:S(2)}) collective-permute-start(f32[8,192]{1,0:T(8,128)S(1)} %bitcast.105), channel_id=1, source_target_pairs={{0,4},{2,6},{4,0},{6,2},{8,12},{10,14},{12,8},{14,10},{16,20},{18,... | collective-permute-start | bytes 18440 | tf_op jit(solution)/shard_map/ppermute | solution.py:251
  60.5 20.9 %collective-permute-start.1 = (bf16[16,64,1024]{2,1,0:T(8,128)(2,1)}, bf16[16,64,1024]{2,1,0:T(8,128)(2,1)S(1)}, u32[]{:S(2)}, u32[]{:S(2)}) collective-permute-start(bf16[16,64,1024]{2,1,0:T(8,128)(2,1)} %all-to-all-done.own.x_1.z_1.own_1), channel_id=1, source_target_pairs={{0,1},{1,0},{2,3},{3,2},{4,5},{5,4},{6,7},{7,6},{8,9},{9,8},{10,11... | collective-permute-start | bytes 6291464 | tf_op jit(solution)/shard_map/ppermute | solution.py:29
  60.5 18.5 %copy-start.6 = (bf16[16,1024]{1,0:T(8,128)(2,1)}, bf16[16,1024]{1,0:T(8,128)(2,1)S(1)}, u32[]{:S(2)}) copy-start(bf16[16,1024]{1,0:T(8,128)(2,1)S(1)} %convert_bitcast_fusion.router_own) | copy-start | bytes 98308
  60.6 7.8 %collective-permute-start.5 = (f32[8,192]{1,0:T(8,128)S(1)}, f32[8,192]{1,0:T(8,128)S(1)}, u32[]{:S(2)}, u32[]{:S(2)}) collective-permute-start(f32[8,192]{1,0:T(8,128)S(1)} %bitcast.106), channel_id=1, source_target_pairs={{0,8},{2,10},{4,12},{6,14},{8,0},{10,2},{12,4},{14,6},{16,24},{18,... | collective-permute-start | bytes 18440 | tf_op jit(solution)/shard_map/ppermute | solution.py:251
  68.5 10.6 %collective-permute-start.6 = (f32[8,192]{1,0:T(8,128)S(1)}, f32[8,192]{1,0:T(8,128)S(1)}, u32[]{:S(2)}, u32[]{:S(2)}) collective-permute-start(f32[8,192]{1,0:T(8,128)S(1)} %bitcast.104), channel_id=1, source_target_pairs={{0,16},{2,18},{4,20},{6,22},{8,24},{10,26},{12,28},{14,30},{16,0},... | collective-permute-start | bytes 18440 | tf_op jit(solution)/shard_map/ppermute | solution.py:251
  74.2 28.5 %all-to-all-start.1 = ((bf16[16,32,1024]{2,1,0:T(8,128)(2,1)}), bf16[16,32,1024]{2,1,0:T(8,128)(2,1)}, u32[]{:S(2)}, u32[]{:S(2)}) async-start(bf16[16,32,1024]{2,1,0:T(8,128)(2,1)} %fill_slots.3), calls=%async_computation.1 | async-start | bytes 2097152 | tf_op jit(solution)/shard_map/all_to_all | solution.py:75
  79.0 2.4 %collective-permute-start.7 = (bf16[16,1024]{1,0:T(8,128)(2,1)S(1)}, bf16[16,1024]{1,0:T(8,128)(2,1)S(1)}, u32[]{:S(2)}, u32[]{:S(2)}) collective-permute-start(bf16[16,1024]{1,0:T(8,128)(2,1)S(1)} %convert_bitcast_fusion.router_own), channel_id=1, source_target_pairs={{0,1},{1,0},{2,3},{3,2},{4,5},{5,4},{6,7},{7,6},{8,9},{9,8},{10,11... | collective-permute-start | bytes 98312 | tf_op jit(solution)/shard_map/ppermute | solution.py:29
  81.4 0.6 copy-start.8
  81.4 1.3 copy-start
  95.4 7.3 %collective-permute-start.8 = (bf16[512,1024]{1,0:T(8,128)(2,1)}, bf16[512,1024]{1,0:T(8,128)(2,1)S(1)}, u32[]{:S(2)}, u32[]{:S(2)}) collective-permute-start(bf16[512,1024]{1,0:T(8,128)(2,1)} %get-tuple-element.36), channel_id=1, source_target_pairs={{0,1},{1,0},{2,3},{3,2},{4,5},{5,4},{6,7},{7,6},{8,9},{9,8},{10,11... | collective-permute-start | bytes 3145736 | tf_op jit(solution)/shard_map/ppermute | solution.py:29
  102.7 10.4 %collective-permute-start.9 = (bf16[16,32,1024]{2,1,0:T(8,128)(2,1)}, bf16[16,32,1024]{2,1,0:T(8,128)(2,1)S(1)}, u32[]{:S(2)}, u32[]{:S(2)}) collective-permute-start(bf16[16,32,1024]{2,1,0:T(8,128)(2,1)} %all-to-all-done.1.own.x_2.z_2.own_2), channel_id=1, source_target_pairs={{0,1},{1,0},{2,3},{3,2},{4,5},{5,4},{6,7},{7,6},{8,9},{9,8},{10,11... | collective-permute-start | bytes 3145736 | tf_op jit(solution)/shard_map/ppermute | solution.py:29
  105.3 30.7 %all-to-all-start.2 = ((bf16[16,32,1024]{2,1,0:T(8,128)(2,1)}), bf16[16,32,1024]{2,1,0:T(8,128)(2,1)S(1)}, u32[]{:S(2)}, u32[]{:S(2)}) async-start(bf16[16,32,1024]{2,1,0:T(8,128)(2,1)} %bitcast.30), calls=%async_computation.2 | async-start | bytes 2097152 | tf_op jit(solution)/shard_map/all_to_all | solution.py:75
  113.1 1.0 copy-start.1
  122.8 2.2 %collective-permute-start.10 = (bf16[256,1024]{1,0:T(8,128)(2,1)}, bf16[256,1024]{1,0:T(8,128)(2,1)S(1)}, u32[]{:S(2)}, u32[]{:S(2)}) collective-permute-start(bf16[256,1024]{1,0:T(8,128)(2,1)} %get-tuple-element.40), channel_id=1, source_target_pairs={{0,1},{1,0},{2,3},{3,2},{4,5},{5,4},{6,7},{7,6},{8,9},{9,8},{10,11... | collective-permute-start | bytes 1572872 | tf_op jit(solution)/shard_map/ppermute | solution.py:29
  136.0 29.8 %all-to-all-start.3 = ((bf16[16,16,1024]{2,1,0:T(8,128)(2,1)}), bf16[16,16,1024]{2,1,0:T(8,128)(2,1)S(1)}, u32[]{:S(2)}, u32[]{:S(2)}) async-start(bf16[16,16,1024]{2,1,0:T(8,128)(2,1)} %bitcast.32), calls=%async_computation.3 | async-start | bytes 1048576 | tf_op jit(solution)/shard_map/all_to_all | solution.py:75
  146.0 5.8 %collective-permute-start.12 = (f32[16,1024]{1,0:T(8,128)}, f32[16,1024]{1,0:T(8,128)S(1)}, u32[]{:S(2)}, u32[]{:S(2)}) collective-permute-start(f32[16,1024]{1,0:T(8,128)} %get-tuple-element.60), channel_id=1, source_target_pairs={{0,1},{1,0},{2,3},{3,2},{4,5},{5,4},{6,7},{7,6},{8,9},{9,8},{10,11... | collective-permute-start | bytes 196616 | tf_op jit(solution)/shard_map/ppermute | solution.py:29
  146.0 5.8 %copy-start.5 = (f32[16,1024]{1,0:T(8,128)S(1)}, f32[16,1024]{1,0:T(8,128)}, u32[]{:S(2)}) copy-start(f32[16,1024]{1,0:T(8,128)} %get-tuple-element.59) | copy-start | bytes 196612
  151.9 9.4 %collective-permute-start.15 = (f32[16,1024]{1,0:T(8,128)S(1)}, f32[16,1024]{1,0:T(8,128)S(1)}, u32[]{:S(2)}, u32[]{:S(2)}) collective-permute-start(f32[16,1024]{1,0:T(8,128)S(1)} %add.160), channel_id=1, source_target_pairs={{0,6},{2,4},{4,2},{6,0},{8,14},{10,12},{12,10},{14,8},{16,22},{18,... | collective-permute-start | bytes 196616 | tf_op jit(solution)/shard_map/ppermute | solution.py:233
  154.8 6.5 %collective-permute-start.14 = (f32[16,1024]{1,0:T(8,128)S(1)}, f32[16,1024]{1,0:T(8,128)S(1)}, u32[]{:S(2)}, u32[]{:S(2)}) collective-permute-start(f32[16,1024]{1,0:T(8,128)S(1)} %add.160), channel_id=1, source_target_pairs={{0,4},{2,6},{4,0},{6,2},{8,12},{10,14},{12,8},{14,10},{16,20},{18,... | collective-permute-start | bytes 196616 | tf_op jit(solution)/shard_map/ppermute | solution.py:233
  155.4 6.0 %collective-permute-start.13 = (f32[16,1024]{1,0:T(8,128)S(1)}, f32[16,1024]{1,0:T(8,128)S(1)}, u32[]{:S(2)}, u32[]{:S(2)}) collective-permute-start(f32[16,1024]{1,0:T(8,128)S(1)} %add.160), channel_id=1, source_target_pairs={{0,2},{2,0},{4,6},{6,4},{8,10},{10,8},{12,14},{14,12},{16,18},{18,... | collective-permute-start | bytes 196616 | tf_op jit(solution)/shard_map/ppermute | solution.py:233
  155.5 10.7 %copy-start.2 = (bf16[256,1024]{1,0:T(8,128)(2,1)S(1)}, bf16[256,1024]{1,0:T(8,128)(2,1)}, u32[]{:S(2)}) copy-start(bf16[256,1024]{1,0:T(8,128)(2,1)} %param.10) | copy-start | bytes 1572868
  161.4 6.5 %collective-permute-start.18 = (f32[16,1024]{1,0:T(8,128)S(1)}, f32[16,1024]{1,0:T(8,128)S(1)}, u32[]{:S(2)}, u32[]{:S(2)}) collective-permute-start(f32[16,1024]{1,0:T(8,128)S(1)} %add_add_fusion.1), channel_id=1, source_target_pairs={{0,24},{2,26},{4,28},{6,30},{8,16},{10,18},{12,20},{14,22},{16,8},... | collective-permute-start | bytes 196616 | tf_op jit(solution)/shard_map/ppermute | solution.py:233
  165.2 5.5 %collective-permute-start.17 = (f32[16,1024]{1,0:T(8,128)S(1)}, f32[16,1024]{1,0:T(8,128)S(1)}, u32[]{:S(2)}, u32[]{:S(2)}) collective-permute-start(f32[16,1024]{1,0:T(8,128)S(1)} %add_add_fusion.1), channel_id=1, source_target_pairs={{0,16},{2,18},{4,20},{6,22},{8,24},{10,26},{12,28},{14,30},{16,0},... | collective-permute-start | bytes 196616 | tf_op jit(solution)/shard_map/ppermute | solution.py:233
  165.2 5.5 %collective-permute-start.16 = (f32[16,1024]{1,0:T(8,128)S(1)}, f32[16,1024]{1,0:T(8,128)S(1)}, u32[]{:S(2)}, u32[]{:S(2)}) collective-permute-start(f32[16,1024]{1,0:T(8,128)S(1)} %add_add_fusion.1), channel_id=1, source_target_pairs={{0,8},{2,10},{4,12},{6,14},{8,0},{10,2},{12,4},{14,6},{16,24},{18,... | collective-permute-start | bytes 196616 | tf_op jit(solution)/shard_map/ppermute | solution.py:233
  166.2 5.1 %copy-start.3 = (bf16[256,1024]{1,0:T(8,128)(2,1)S(1)}, bf16[256,1024]{1,0:T(8,128)(2,1)}, u32[]{:S(2)}) copy-start(bf16[256,1024]{1,0:T(8,128)(2,1)} %param.11) | copy-start | bytes 1572868
  166.9 4.4 %collective-permute-start.11 = (f32[2,256]{1,0:T(2,128)S(1)}, f32[2,256]{1,0:T(2,128)S(1)}, u32[]{:S(2)}, u32[]{:S(2)}) collective-permute-start(f32[2,256]{1,0:T(2,128)S(1)} %pad_maximum_fusion.8), channel_id=1, source_target_pairs={{0,1},{1,0},{2,3},{3,2},{4,5},{5,4},{6,7},{7,6},{8,9},{9,8},{10,11... | collective-permute-start | bytes 6152 | tf_op jit(solution)/shard_map/ppermute | solution.py:29
where the time goes:
time: 173 us
  waiting for transfers between devices  58.8 us (34%)
  starting transfers between devices  50.6 us (29%)
  Pallas kernels  39.6 us (23%)
  other arithmetic  14.4 us (8%)
  local copies, waits for them, and re-layouts  5.88 us (3%)
  matrix products  2.11 us (1%)
    all_to_all x4, waiting for transfers between devices, all_to_all(): return lax.all_to_all(value, 'dp', split_axis=0, concat_axis=0, tiled=True)  47.4 us
    all_to_all x4, starting transfers between devices, all_to_all(): return lax.all_to_all(value, 'dp', split_axis=0, concat_axis=0, tiled=True)  25.6 us
    pallas_call x2, Pallas kernels, expert_rows(): pl.pallas_call(expert_body, name='expert_rows', in_specs=[pl.BlockSpec(me...  21.3 us
    ppermute x4, starting transfers between devices, dp_exchange(): other = lax.ppermute(sent, 'dp', [(i, i ^ step) for i in range(size)])  15.3 us
    pallas_call x2, Pallas kernels, weight_grads(): pl.pallas_call(weight_body, name='weight_grads', grid_spec=pltpu.Prefetch...  11.7 us
    ppermute x6, starting transfers between devices, dp_total(): lax.ppermute(value, 'dp', [(i, i ^ step * k) for i in range(size)])  8.01 us
    ppermute x4, waiting for transfers between devices, dp_exchange(): other = lax.ppermute(sent, 'dp', [(i, i ^ step) for i in range(size)])  4.91 us
    convert_element_type x2, other arithmetic, per_device(): (part_own.astype(F32) + pair_swap(part_oth).astype(F32)).astype(BF16)  4.59 us
  transfers between devices with their start and end apart: 23, of which 9 were waited for; matrix products, arithmetic and copies ran while one was open for 9% of the time, Pallas kernels for 22%

commit v1 on v0

--- a/solution.py
+++ b/solution.py
@@ -226,7 +226,7 @@
         return dp_sum(value)
     step = 1
     while step < size:
-        far = 3 if step * 2 < size else 1
+        far = 3 if step == 1 else 1
         others = []
         for k in range(1, far + 1):
             others.append(
@@ -488,6 +488,56 @@
     )(targets, x_rows, z_rows)
 
 
+def token_body(
+    routes, own_sums, oth_sums, latents, cotangent, shift, scale, gate,
+    out, normed_b, scaled_dy, targets,
+):
+    experts, span, width = out.shape
+    chunk = span // 2
+    tokens = routes.shape[1]
+    capacity = 3 * tokens // experts
+    expert_ids = lax.broadcasted_iota(jnp.int32, (experts, tokens), 0)
+    named = [jnp.where(routes[k:k + 1, :] == expert_ids, 1.0, 0.0) for k in range(2)]
+    rows_i = lax.broadcasted_iota(jnp.int32, (tokens, tokens), 0)
+    cols_i = lax.broadcasted_iota(jnp.int32, (tokens, tokens), 1)
+    earlier = jnp.where(rows_i < cols_i, 1.0, 0.0).astype(BF16)
+    places = lin((named[0] + named[1]).astype(BF16), earlier)
+    places = places + (expert_ids * capacity).astype(F32)
+    for k in range(2):
+        targets[k:k + 1, :] = jnp.sum(named[k] * places, axis=0, keepdims=True)
+    sums = (own_sums[...] + oth_sums[...]) / (2 * width)
+    inv_std = lax.rsqrt(sums[1:2] - sums[0:1] * sums[0:1] + norm_eps)
+
+    def column(row):
+        return jnp.broadcast_to(row, (8, tokens)).T[:, 0:1]
+
+    normed = (latents[...].astype(F32) - column(sums[0:1])) * column(inv_std)
+    normed = normed * (1.0 + scale[...].astype(F32)) + shift[...].astype(F32)
+    x_rows = normed.astype(BF16)
+    z_rows = (gate[...].astype(F32) * cotangent[...].astype(F32)).astype(BF16)
+    normed_b[...] = x_rows
+    scaled_dy[...] = z_rows
+    index = lax.broadcasted_iota(jnp.int32, (experts * chunk, tokens), 0)
+    ids = (index // chunk * capacity + index % chunk).astype(F32)
+    hit = (targets[0:1, :] == ids) | (targets[1:2, :] == ids)
+    fill = jnp.where(hit, 1.0, 0.0).astype(BF16)
+    out[:, :chunk, :] = lin(fill, x_rows).astype(BF16).reshape(experts, chunk, width)
+    out[:, chunk:, :] = lin(fill, z_rows).astype(BF16).reshape(experts, chunk, width)
+
+
+def token_slots(routes, own_sums, oth_sums, latents, cotangent, shift, scale, gate, experts, chunk):
+    tokens, width = latents.shape
+    rows = jax.ShapeDtypeStruct((tokens, width), BF16)
+    return pl.pallas_call(
+        token_body,
+        name="token_slots",
+        out_shape=[
+            jax.ShapeDtypeStruct((experts, 2 * chunk, width), BF16), rows, rows,
+            jax.ShapeDtypeStruct(routes.shape, F32),
+        ],
+    )(routes, own_sums, oth_sums, latents, cotangent, shift, scale, gate)
+
+
 def per_device(
     latents, cotangent, routes, router_w, mod_shift, mod_scale, mod_gate, gate_w, up_w, down_w
 ):
@@ -507,33 +557,37 @@
     core = lax.axis_index("expert").astype(jnp.int32).reshape(1)
     gate_w, up_w, down_w = gate_w[0], up_w[0], down_w[0]
 
+    first = capacity // 3 * 2
+    parts = ((0, first), (first, capacity - first))
+
+    def slot_of(index, first, length):
+        return (index // length * capacity + index % length + first).astype(F32)
+
+    def mod_row(table):
+        return lax.dynamic_slice_in_dim(table, sample_index, 1, 0)
+
+    x = latents.astype(F32)
+    own_sums = jnp.stack([jnp.sum(x, axis=1), jnp.sum(x * x, axis=1)])
+    oth_sums = pair_swap(own_sums)
+    second = capacity - first
+    send_1, normed_b, scaled_dy, targets = token_slots(
+        routes.T, own_sums, oth_sums, latents, cotangent,
+        mod_row(mod_shift), mod_row(mod_scale), mod_row(mod_gate), experts, first,
+    )
+    own_sums, latents, mod_shift, mod_scale, routes, _ = lax.optimization_barrier(
+        (own_sums, latents, mod_shift, mod_scale, routes, send_1)
+    )
     expert_ids = lax.broadcasted_iota(jnp.int32, (experts, tok_rows), 0)
     named = [routes[:, k][None, :] == expert_ids for k in range(2)]
-    named_b = (named[0] | named[1]).astype(BF16)
-    rows_i = lax.broadcasted_iota(jnp.int32, (tok_rows, tok_rows), 0)
-    cols_i = lax.broadcasted_iota(jnp.int32, (tok_rows, tok_rows), 1)
-    places = lin(named_b, (rows_i < cols_i).astype(BF16)) + (expert_ids * capacity).astype(F32)
-    targets = [jnp.sum(jnp.where(n, places, 0.0), axis=0) for n in named]
-    first = capacity // 3 * 2
-    parts = ((0, first), (first, capacity - first))
-
-    def slot_of(index, first, length):
-        return (index // length * capacity + index % length + first).astype(F32)
-
     cot = cotangent.astype(F32)
-    scaled_dy = (selected_row(mod_gate, sample_index) * cot).astype(BF16)
     x = latents.astype(F32)
-    sums = jnp.stack([jnp.sum(x, axis=1), jnp.sum(x * x, axis=1)])
-    mean, msq = core_sum(sums) / entire_width
+    mean, msq = (own_sums + oth_sums) / entire_width
     inv_std = lax.rsqrt(msq - mean * mean + norm_eps)[:, None]
     xhat = (x - mean[:, None]) * inv_std
     amp = 1.0 + selected_row(mod_scale, sample_index)
     normed = xhat * amp + selected_row(mod_shift, sample_index)
-    normed_b = normed.astype(BF16)
-    second = capacity - first
-    send_1 = fill_slots(jnp.stack(targets), normed_b, scaled_dy, experts, 0, first)
     send_2 = fill_slots(
-        after(jnp.stack(targets), send_1), normed_b, scaled_dy, experts, first, second
+        targets, normed_b, scaled_dy, experts, first, second
     )
     own_1 = all_to_all(send_1)
     own_2 = all_to_all(send_2)

time: 173 us -> 172 us (level)
  other arithmetic: 14.4 us -> 11.8 us
    pallas_call x0 -> x1, Pallas kernels: none -> 3.68 us  [token_slots(): pl.pallas_call(token_body, name='token_slots', out_shape=[jax.ShapeDtypeS...]
    ppermute x9, waiting for transfers between devices: 2.86 us -> 5.28 us  [pair_swap(): return lax.ppermute(value, 'expert', [(0, 1), (1, 0)])]
    pallas_call x2 -> x1, Pallas kernels: 3.46 us -> 1.41 us  [fill_slots(): pl.pallas_call(functools.partial(fill_body, first), name='fill_slots', co...]
    add x2, other arithmetic: 2.29 us -> 0.29 us  [per_device(): normed = xhat * amp + selected_row(mod_shift, sample_index)]
    ppermute x6 -> x5, waiting for transfers between devices: 3.66 us -> 1.9 us  [dp_total(): lax.ppermute(value, 'dp', [(i, i ^ step * k) for i in range(size)])]
    ppermute x6 -> x5, starting transfers between devices: 8.01 us -> 7.97 us  [dp_total(): lax.ppermute(value, 'dp', [(i, i ^ step * k) for i in range(size)])]
  transfers between devices with their start and end apart: 23 -> 22, of which waited for: 9 -> 10; matrix products, arithmetic and copies ran while one was open for 9% -> 8% of each run, Pallas kernels for 22% -> 22%
where the time goes in v1:
time: 172 us; the launch traced here: 171 us
  waiting for transfers between devices  59.3 us (34%)
  starting transfers between devices  50 us (29%)
  Pallas kernels  41.2 us (24%)
  other arithmetic  11.8 us (7%)
  local copies, waits for them, and re-layouts  5.75 us (3%)
  matrix products  1.95 us (1%)
    all_to_all x4, waiting for transfers between devices, all_to_all(): return lax.all_to_all(value, 'dp', split_axis=0, concat_axis=0, tiled=True)  48 us
    all_to_all x4, starting transfers between devices, all_to_all(): return lax.all_to_all(value, 'dp', split_axis=0, concat_axis=0, tiled=True)  25.7 us
    pallas_call x2, Pallas kernels, expert_rows(): pl.pallas_call(expert_body, name='expert_rows', in_specs=[pl.BlockSpec(me...  21.3 us
    ppermute x4, starting transfers between devices, dp_exchange(): other = lax.ppermute(sent, 'dp', [(i, i ^ step) for i in range(size)])  14.8 us
    pallas_call x2, Pallas kernels, weight_grads(): pl.pallas_call(weight_body, name='weight_grads', grid_spec=pltpu.Prefetch...  11.6 us
    ppermute x5, starting transfers between devices, dp_total(): lax.ppermute(value, 'dp', [(i, i ^ step * k) for i in range(size)])  7.97 us
    ppermute x9, waiting for transfers between devices, pair_swap(): return lax.ppermute(value, 'expert', [(0, 1), (1, 0)])  5.28 us
    convert_element_type x2, other arithmetic, per_device(): (part_own.astype(F32) + pair_swap(part_oth).astype(F32)).astype(BF16)  4.63 us
  transfers between devices with their start and end apart: 22, of which 10 were waited for; matrix products, arithmetic and copies ran while one was open for 8% of the time, Pallas kernels for 22%

profile of v1, /device:TPU:0, one launch (start us, length us, event | category | flops | bytes accessed | tf_op | source)
XLA Modules:
  0.0 171.3 jit_solution(5451404524319123986)
XLA Ops:
  0.6 1.3 convert_reduce_fusion
  1.9 0.6 collective-permute-start
  2.5 0.8 collective-permute-done.oth_sums
  3.3 0.6 copy-done.15
  3.9 3.7 %token_slots.1 = (bf16[16,64,1024]{2,1,0:T(8,128)(2,1)}, bf16[256,1024]{1,0:T(8,128)(2,1)}, bf16[256,1024]{1,0:T(8,128)(2,1)}, f32[2,256]{1,0:T(2,128)}) custom-call(s32[2,256]{1,0:T(2,128)} %bitcast.86, f32[2,256]{1,0:T(2,128)} %copy-done.10, f32[2,256]{1,0:T(2,128)} %copy-done.15, bf16[256,1024]{1,0:T(8,128)(2,1)} %latents.1, bf16[256,1024]{1,0:T(8,128)(2,1)} %cotangent.1, ...), custom_call_target="tpu_custom_call" | custom-call | tf_op jit(solution)/shard_map/token_slots/pallas_call | solution.py:531
  7.7 8.4 %all-to-all-start = ((bf16[16,64,1024]{2,1,0:T(8,128)(2,1)}), bf16[16,64,1024]{2,1,0:T(8,128)(2,1)}, u32[]{:S(2)}, u32[]{:S(2)}) async-start(bf16[16,64,1024]{2,1,0:T(8,128)(2,1)} %get-tuple-element.41), calls=%async_computation | async-start | bytes 4194304 | tf_op jit(solution)/shard_map/all_to_all | solution.py:75
  16.1 0.1 rev.8
  16.3 0.3 multiply_add_fusion
  16.6 0.9 convolution_bitcast_fusion
  17.6 1.1 collective-permute-done.2
  18.8 0.1 rev.7
  18.9 0.6 fusion.5
  19.5 0.1 concatenate.25
  19.6 0.1 concatenate.26
  19.7 0.1 concatenate.24
  19.7 0.1 concatenate.27
  19.8 0.1 pad_maximum_fusion
  20.0 1.9 %collective-permute-start.3 = (f32[8,192]{1,0:T(8,128)S(1)}, f32[8,192]{1,0:T(8,128)S(1)}, u32[]{:S(2)}, u32[]{:S(2)}) collective-permute-start(f32[8,192]{1,0:T(8,128)S(1)} %bitcast.108), channel_id=1, source_target_pairs={{0,2},{2,0},{4,6},{6,4},{8,10},{10,8},{12,14},{14,12},{16,18},{18,... | collective-permute-start | bytes 18440 | tf_op jit(solution)/shard_map/ppermute | solution.py:251
  21.9 2.5 %collective-permute-done.3 = f32[8,192]{1,0:T(8,128)S(1)} collective-permute-done((f32[8,192]{1,0:T(8,128)S(1)}, f32[8,192]{1,0:T(8,128)S(1)}, u32[]{:S(2)}, u32[]{:S(2)}) %collective-permute-start.3) | collective-permute-done | bytes 6176 | tf_op jit(solution)/shard_map/ppermute | solution.py:251
  24.5 2.7 %collective-permute-start.4 = (f32[8,192]{1,0:T(8,128)S(1)}, f32[8,192]{1,0:T(8,128)S(1)}, u32[]{:S(2)}, u32[]{:S(2)}) collective-permute-start(f32[8,192]{1,0:T(8,128)S(1)} %bitcast.106), channel_id=1, source_target_pairs={{0,4},{2,6},{4,0},{6,2},{8,12},{10,14},{12,8},{14,10},{16,20},{18,... | collective-permute-start | bytes 18440 | tf_op jit(solution)/shard_map/ppermute | solution.py:251
  27.2 32.2 %all-to-all-done.own.x_1.z_1.own_1 = bf16[16,64,1024]{2,1,0:T(8,128)(2,1)} async-done(((bf16[16,64,1024]{2,1,0:T(8,128)(2,1)}), bf16[16,64,1024]{2,1,0:T(8,128)(2,1)}, u32[]{:S(2)}, u32[]{:S(2)}) %all-to-all-start) | async-done | bytes 2097184 | tf_op jit(solution)/shard_map/all_to_all | solution.py:75
  59.5 6.2 %collective-permute-start.5 = (f32[8,192]{1,0:T(8,128)S(1)}, f32[8,192]{1,0:T(8,128)S(1)}, u32[]{:S(2)}, u32[]{:S(2)}) collective-permute-start(f32[8,192]{1,0:T(8,128)S(1)} %bitcast.107), channel_id=1, source_target_pairs={{0,8},{2,10},{4,12},{6,14},{8,0},{10,2},{12,4},{14,6},{16,24},{18,... | collective-permute-start | bytes 18440 | tf_op jit(solution)/shard_map/ppermute | solution.py:251
  65.7 1.6 collective-permute-done.5
  67.4 4.0 %collective-permute-start.6 = (f32[8,192]{1,0:T(8,128)S(1)}, f32[8,192]{1,0:T(8,128)S(1)}, u32[]{:S(2)}, u32[]{:S(2)}) collective-permute-start(f32[8,192]{1,0:T(8,128)S(1)} %bitcast.105), channel_id=1, source_target_pairs={{0,16},{2,18},{4,20},{6,22},{8,24},{10,26},{12,28},{14,30},{16,0},... | collective-permute-start | bytes 18440 | tf_op jit(solution)/shard_map/ppermute | solution.py:251
  71.3 1.4 fill_slots.1
  72.8 4.6 %all-to-all-start.1 = ((bf16[16,32,1024]{2,1,0:T(8,128)(2,1)}), bf16[16,32,1024]{2,1,0:T(8,128)(2,1)}, u32[]{:S(2)}, u32[]{:S(2)}) async-start(bf16[16,32,1024]{2,1,0:T(8,128)(2,1)} %fill_slots.1), calls=%async_computation.1 | async-start | bytes 2097152 | tf_op jit(solution)/shard_map/all_to_all | solution.py:75
  77.6 0.1 eq.140
  77.6 0.1 broadcast_in_dim.136
  77.8 1.0 select_subtract_fusion.coefs
  78.8 1.0 reshape.128.slot_w
  79.8 0.6 copy-done.17
  80.4 0.7 copy-done.3
  81.1 12.6 %expert_rows.2 = (bf16[512,1024]{1,0:T(8,128)(2,1)}, bf16[512,1024]{1,0:T(8,128)(2,1)}, bf16[512,512]{1,0:T(8,128)(2,1)}, bf16[512,512]{1,0:T(8,128)(2,1)}, bf16...) custom-call(s32[1]{0:T(128)} %bitcast.7.core, ...), custom_call_target="tpu_custom_call" | custom-call | flops 5368709120 | bytes 14155776 | tf_op jit(solution)/shard_map/expert_rows/pallas_call | solution.py:349
  93.7 0.6 collective-permute-start.8
  94.3 6.8 %all-to-all-done.1.own.x_2.z_2.own_2 = bf16[16,32,1024]{2,1,0:T(8,128)(2,1)} async-done(((bf16[16,32,1024]{2,1,0:T(8,128)(2,1)}), bf16[16,32,1024]{2,1,0:T(8,128)(2,1)}, u32[]{:S(2)}, u32[]{:S(2)}) %all-to-all-start.1) | async-done | bytes 1048608 | tf_op jit(solution)/shard_map/all_to_all | solution.py:75
  101.0 2.6 %add_convert_fusion = bf16[512,1024]{1,0:T(8,128)(2,1)} fusion(bf16[512,1024]{1,0:T(8,128)(2,1)S(1)} %collective-permute-done.8, bf16[512,1024]{1,0:T(8,128)(2,1)} %get-tuple-element.50), kind=kLoop, calls=%fused_computation | loop fusion | flops 2097152 | bytes 3145728 | tf_op jit(solution)/shard_map/convert_element_type | solution.py:641
  103.6 5.9 %all-to-all-start.2 = ((bf16[16,32,1024]{2,1,0:T(8,128)(2,1)}), bf16[16,32,1024]{2,1,0:T(8,128)(2,1)S(1)}, u32[]{:S(2)}, u32[]{:S(2)}) async-start(bf16[16,32,1024]{2,1,0:T(8,128)(2,1)} %bitcast.30), calls=%async_computation.2 | async-start | bytes 2097152 | tf_op jit(solution)/shard_map/all_to_all | solution.py:75
  109.6 0.1 eq.147
  109.7 0.1 broadcast_in_dim.141
  109.8 0.1 broadcast_in_dim.144
  109.8 0.8 reshape.129.slot_w
  110.6 0.8 select_subtract_fusion.1.coefs
  111.4 1.0 copy-done.4
  112.4 8.7 %expert_rows.3 = (bf16[256,1024]{1,0:T(8,128)(2,1)}, bf16[256,1024]{1,0:T(8,128)(2,1)}, bf16[256,512]{1,0:T(8,128)(2,1)}, bf16[256,512]{1,0:T(8,128)(2,1)}, bf16...) custom-call(s32[1]{0:T(128)} %bitcast.7.core, ...), custom_call_target="tpu_custom_call" | custom-call | flops 2684354560 | bytes 10223616 | tf_op jit(solution)/shard_map/expert_rows/pallas_call | solution.py:349
  121.1 0.3 collective-permute-start.10
  121.4 1.9 %collective-permute-done.10 = bf16[256,1024]{1,0:T(8,128)(2,1)S(1)} collective-permute-done((bf16[256,1024]{1,0:T(8,128)(2,1)}, bf16[256,1024]{1,0:T(8,128)(2,1)S(1)}, u32[]{:S(2)}, u32[]{:S(2)}) %collective-permute-start.10) | collective-permute-done | bytes 524320 | tf_op jit(solution)/shard_map/ppermute | solution.py:29
  123.3 2.0 %add_convert_fusion.2 = bf16[256,1024]{1,0:T(8,128)(2,1)} fusion(bf16[256,1024]{1,0:T(8,128)(2,1)S(1)} %collective-permute-done.10, bf16[256,1024]{1,0:T(8,128)(2,1)} %get-tuple-element.55), kind=kLoop, calls=%fused_computation.17 | loop fusion | flops 1048576 | bytes 1572864 | tf_op jit(solution)/shard_map/convert_element_type | solution.py:647
  125.3 9.1 %all-to-all-done.2 = bf16[16,32,1024]{2,1,0:T(8,128)(2,1)S(1)} async-done(((bf16[16,32,1024]{2,1,0:T(8,128)(2,1)}), bf16[16,32,1024]{2,1,0:T(8,128)(2,1)S(1)}, u32[]{:S(2)}, u32[]{:S(2)}) %all-to-all-start.2) | async-done | bytes 1048608 | tf_op jit(solution)/shard_map/all_to_all | solution.py:75
  134.4 6.8 %all-to-all-start.3 = ((bf16[16,16,1024]{2,1,0:T(8,128)(2,1)}), bf16[16,16,1024]{2,1,0:T(8,128)(2,1)S(1)}, u32[]{:S(2)}, u32[]{:S(2)}) async-start(bf16[16,16,1024]{2,1,0:T(8,128)(2,1)} %bitcast.32), calls=%async_computation.3 | async-start | bytes 1048576 | tf_op jit(solution)/shard_map/all_to_all | solution.py:75
  141.2 3.2 %router_grads.1 = (f32[16,1024]{1,0:T(8,128)}, f32[16,1024]{1,0:T(8,128)}) custom-call(bf16[16,64,1024]{2,1,0:T(8,128)(2,1)} %all-to-all-done.own.x_1.z_1.own_1, bf16[16,64,1024]{2,1,0:T(8,128)(2,1)} %copy-done.3, bf16[16,32,1024]{2,1,0:T(8,128)(2,1)} %all-to-all-done.1.own.x_2.z_2.own_2, bf16[16,32,1024]{2,1,0:T(8,128)(2,1)} %copy-done.4, ...), custom_call_target="tpu_custom_call" | custom-call | flops 100663296 | bytes 3145728 | tf_op jit(solution)/shard_map/router_grads/pallas_call | solution.py:401
  144.4 1.4 collective-permute-done.12
  145.8 0.8 add.155
  146.7 2.9 %collective-permute-start.15 = (f32[16,1024]{1,0:T(8,128)S(1)}, f32[16,1024]{1,0:T(8,128)S(1)}, u32[]{:S(2)}, u32[]{:S(2)}) collective-permute-start(f32[16,1024]{1,0:T(8,128)S(1)} %add.155), channel_id=1, source_target_pairs={{0,6},{2,4},{4,2},{6,0},{8,14},{10,12},{12,10},{14,8},{16,22},{18,... | collective-permute-start | bytes 196616 | tf_op jit(solution)/shard_map/ppermute | solution.py:233
  149.6 0.6 collective-permute-start.14
  150.1 0.1 collective-permute-start.13
  150.2 5.8 %weight_grads.2 = (bf16[2048,512]{1,0:T(8,128)(2,1)}, bf16[2048,512]{1,0:T(8,128)(2,1)}, bf16[512,2048]{1,0:T(8,128)(2,1)}) custom-call(s32[1]{0:T(128)} %bitcast.7.core, bf16[16,64,1024]{2,1,0:T(8,128)(2,1)} %all-to-all-done.own.x_1.z_1.own_1, bf16[16,64,1024]{2,1,0:T(8,128)(2,1)} %all-to-all-done.own.x_1.z_1.own_1, ...), custom_call_target="tpu_custom_call" | custom-call | flops 2415919104 | bytes 8650752 | tf_op jit(solution)/shard_map/weight_grads/pallas_call | solution.py:446
  156.1 2.0 %collective-permute-start.16 = (f32[16,1024]{1,0:T(8,128)S(1)}, f32[16,1024]{1,0:T(8,128)S(1)}, u32[]{:S(2)}, u32[]{:S(2)}) collective-permute-start(f32[16,1024]{1,0:T(8,128)S(1)} %add_add_fusion.1), channel_id=1, source_target_pairs={{0,8},{2,10},{4,12},{6,14},{8,0},{10,2},{12,4},{14,6},{16,24},{18,... | collective-permute-start | bytes 196616 | tf_op jit(solution)/shard_map/ppermute | solution.py:233
  158.1 5.8 %weight_grads.3 = (bf16[2048,512]{1,0:T(8,128)(2,1)}, bf16[2048,512]{1,0:T(8,128)(2,1)}, bf16[512,2048]{1,0:T(8,128)(2,1)}) custom-call(s32[1]{0:T(128)} %bitcast.7.core, bf16[16,64,1024]{2,1,0:T(8,128)(2,1)} %copy-done.3, bf16[16,64,1024]{2,1,0:T(8,128)(2,1)} %copy-done.3, ...), custom_call_target="tpu_custom_call", output_to_operand_aliasing={{0}: (11, {}), {1}: (12, {}), {2}: (13, {})} | custom-call | flops 2415919104 | bytes 8650752 | tf_op jit(solution)/shard_map/weight_grads/pallas_call | solution.py:446
  163.9 2.4 %collective-permute-start.17 = (f32[16,1024]{1,0:T(8,128)S(1)}, f32[16,1024]{1,0:T(8,128)S(1)}, u32[]{:S(2)}, u32[]{:S(2)}) collective-permute-start(f32[16,1024]{1,0:T(8,128)S(1)} %add.159), channel_id=1, source_target_pairs={{0,16},{2,18},{4,20},{6,22},{8,24},{10,26},{12,28},{14,30},{16,0},... | collective-permute-start | bytes 196616 | tf_op jit(solution)/shard_map/ppermute | solution.py:233
  166.4 0.3 fusion.20
  166.8 0.7 fusion.56
  167.5 1.9 %collective-permute-done.17 = f32[16,1024]{1,0:T(8,128)S(1)} collective-permute-done((f32[16,1024]{1,0:T(8,128)S(1)}, f32[16,1024]{1,0:T(8,128)S(1)}, u32[]{:S(2)}, u32[]{:S(2)}) %collective-permute-start.17) | collective-permute-done | bytes 65568 | tf_op jit(solution)/shard_map/ppermute | solution.py:233
  169.4 0.6 add_bitcast_fusion
  170.1 1.2 add_convert_fusion.1
  (102 shorter events, 0.9 us)
Async XLA Ops:
  1.9 1.4 copy-start.10
  1.9 1.4 collective-permute-start
  3.3 0.6 copy-start.15
  7.6 8.5 %copy-start.12 = (s32[256,2]{0,1:T(2,128)S(1)}, s32[256,2]{0,1:T(2,128)}, u32[]{:S(2)}) copy-start(s32[256,2]{0,1:T(2,128)} %param.12) | copy-start | bytes 6148
  7.6 8.6 %copy-start.13 = (bf16[1,1024]{1,0:T(2,128)(2,1)S(1)}, bf16[1,1024]{1,0:T(2,128)(2,1)}, u32[]{:S(2)}) copy-start(bf16[1,1024]{1,0:T(2,128)(2,1)} %shift) | copy-start | bytes 6148
  7.6 8.6 %copy-start.11 = (f32[2,256]{1,0:T(2,128)S(1)}, f32[2,256]{1,0:T(2,128)}, u32[]{:S(2)}) copy-start(f32[2,256]{1,0:T(2,128)} %copy-done.10) | copy-start | bytes 6148
  7.6 8.6 %copy-start.16 = (f32[2,256]{1,0:T(2,128)S(1)}, f32[2,256]{1,0:T(2,128)}, u32[]{:S(2)}) copy-start(f32[2,256]{1,0:T(2,128)} %copy-done.15) | copy-start | bytes 6148
  7.6 8.7 %copy-start.14 = (bf16[1,1024]{1,0:T(2,128)(2,1)S(1)}, bf16[1,1024]{1,0:T(2,128)(2,1)}, u32[]{:S(2)}) copy-start(bf16[1,1024]{1,0:T(2,128)(2,1)} %scale) | copy-start | bytes 6148
  7.6 8.7 %copy-start.5 = (bf16[256,1024]{1,0:T(8,128)(2,1)S(1)}, bf16[256,1024]{1,0:T(8,128)(2,1)}, u32[]{:S(2)}) copy-start(bf16[256,1024]{1,0:T(8,128)(2,1)} %latents.1) | copy-start | bytes 1572868
  7.6 9.0 %copy-start.8 = (f32[1024,16]{0,1:T(8,128)S(1)}, f32[1024,16]{0,1:T(8,128)}, u32[]{:S(2)}) copy-start(f32[1024,16]{0,1:T(8,128)} %param.13) | copy-start | bytes 196612
  7.7 51.7 %all-to-all-start = ((bf16[16,64,1024]{2,1,0:T(8,128)(2,1)}), bf16[16,64,1024]{2,1,0:T(8,128)(2,1)}, u32[]{:S(2)}, u32[]{:S(2)}) async-start(bf16[16,64,1024]{2,1,0:T(8,128)(2,1)} %get-tuple-element.41), calls=%async_computation | async-start | bytes 4194304 | tf_op jit(solution)/shard_map/all_to_all | solution.py:75
  16.0 1.5 copy-start.2
  16.1 55.3 %copy-start = (bf16[256,1024]{1,0:T(8,128)(2,1)S(1)}, bf16[256,1024]{1,0:T(8,128)(2,1)}, u32[]{:S(2)}) copy-start(bf16[256,1024]{1,0:T(8,128)(2,1)} %get-tuple-element.52.x_rows) | copy-start | bytes 1572868
  16.1 55.3 %copy-start.1 = (bf16[256,1024]{1,0:T(8,128)(2,1)S(1)}, bf16[256,1024]{1,0:T(8,128)(2,1)}, u32[]{:S(2)}) copy-start(bf16[256,1024]{1,0:T(8,128)(2,1)} %get-tuple-element.53.z_rows) | copy-start | bytes 1572868
  17.5 1.2 collective-permute-start.2
  20.0 4.4 %collective-permute-start.3 = (f32[8,192]{1,0:T(8,128)S(1)}, f32[8,192]{1,0:T(8,128)S(1)}, u32[]{:S(2)}, u32[]{:S(2)}) collective-permute-start(f32[8,192]{1,0:T(8,128)S(1)} %bitcast.108), channel_id=1, source_target_pairs={{0,2},{2,0},{4,6},{6,4},{8,10},{10,8},{12,14},{14,12},{16,18},{18,... | collective-permute-start | bytes 18440 | tf_op jit(solution)/shard_map/ppermute | solution.py:251
  24.5 34.9 %collective-permute-start.4 = (f32[8,192]{1,0:T(8,128)S(1)}, f32[8,192]{1,0:T(8,128)S(1)}, u32[]{:S(2)}, u32[]{:S(2)}) collective-permute-start(f32[8,192]{1,0:T(8,128)S(1)} %bitcast.106), channel_id=1, source_target_pairs={{0,4},{2,6},{4,0},{6,2},{8,12},{10,14},{12,8},{14,10},{16,20},{18,... | collective-permute-start | bytes 18440 | tf_op jit(solution)/shard_map/ppermute | solution.py:251
  59.4 20.4 %collective-permute-start.1 = (bf16[16,64,1024]{2,1,0:T(8,128)(2,1)}, bf16[16,64,1024]{2,1,0:T(8,128)(2,1)S(1)}, u32[]{:S(2)}, u32[]{:S(2)}) collective-permute-start(bf16[16,64,1024]{2,1,0:T(8,128)(2,1)} %all-to-all-done.own.x_1.z_1.own_1), channel_id=1, source_target_pairs={{0,1},{1,0},{2,3},{3,2},{4,5},{5,4},{6,7},{7,6},{8,9},{9,8},{10,11... | collective-permute-start | bytes 6291464 | tf_op jit(solution)/shard_map/ppermute | solution.py:29
  59.4 18.0 %copy-start.9 = (bf16[16,1024]{1,0:T(8,128)(2,1)}, bf16[16,1024]{1,0:T(8,128)(2,1)S(1)}, u32[]{:S(2)}) copy-start(bf16[16,1024]{1,0:T(8,128)(2,1)S(1)} %convert_bitcast_fusion.router_own) | copy-start | bytes 98308
  59.5 7.8 %collective-permute-start.5 = (f32[8,192]{1,0:T(8,128)S(1)}, f32[8,192]{1,0:T(8,128)S(1)}, u32[]{:S(2)}, u32[]{:S(2)}) collective-permute-start(f32[8,192]{1,0:T(8,128)S(1)} %bitcast.107), channel_id=1, source_target_pairs={{0,8},{2,10},{4,12},{6,14},{8,0},{10,2},{12,4},{14,6},{16,24},{18,... | collective-permute-start | bytes 18440 | tf_op jit(solution)/shard_map/ppermute | solution.py:251
  67.4 10.1 %collective-permute-start.6 = (f32[8,192]{1,0:T(8,128)S(1)}, f32[8,192]{1,0:T(8,128)S(1)}, u32[]{:S(2)}, u32[]{:S(2)}) collective-permute-start(f32[8,192]{1,0:T(8,128)S(1)} %bitcast.105), channel_id=1, source_target_pairs={{0,16},{2,18},{4,20},{6,22},{8,24},{10,26},{12,28},{14,30},{16,0},... | collective-permute-start | bytes 18440 | tf_op jit(solution)/shard_map/ppermute | solution.py:251
  72.8 28.3 %all-to-all-start.1 = ((bf16[16,32,1024]{2,1,0:T(8,128)(2,1)}), bf16[16,32,1024]{2,1,0:T(8,128)(2,1)}, u32[]{:S(2)}, u32[]{:S(2)}) async-start(bf16[16,32,1024]{2,1,0:T(8,128)(2,1)} %fill_slots.1), calls=%async_computation.1 | async-start | bytes 2097152 | tf_op jit(solution)/shard_map/all_to_all | solution.py:75
  77.4 2.4 %collective-permute-start.7 = (bf16[16,1024]{1,0:T(8,128)(2,1)S(1)}, bf16[16,1024]{1,0:T(8,128)(2,1)S(1)}, u32[]{:S(2)}, u32[]{:S(2)}) collective-permute-start(bf16[16,1024]{1,0:T(8,128)(2,1)S(1)} %convert_bitcast_fusion.router_own), channel_id=1, source_target_pairs={{0,1},{1,0},{2,3},{3,2},{4,5},{5,4},{6,7},{7,6},{8,9},{9,8},{10,11... | collective-permute-start | bytes 98312 | tf_op jit(solution)/shard_map/ppermute | solution.py:29
  79.7 0.6 copy-start.17
  79.8 1.3 copy-start.3
  93.7 7.3 %collective-permute-start.8 = (bf16[512,1024]{1,0:T(8,128)(2,1)}, bf16[512,1024]{1,0:T(8,128)(2,1)S(1)}, u32[]{:S(2)}, u32[]{:S(2)}) collective-permute-start(bf16[512,1024]{1,0:T(8,128)(2,1)} %get-tuple-element.51), channel_id=1, source_target_pairs={{0,1},{1,0},{2,3},{3,2},{4,5},{5,4},{6,7},{7,6},{8,9},{9,8},{10,11... | collective-permute-start | bytes 3145736 | tf_op jit(solution)/shard_map/ppermute | solution.py:29
  101.0 10.4 %collective-permute-start.9 = (bf16[16,32,1024]{2,1,0:T(8,128)(2,1)}, bf16[16,32,1024]{2,1,0:T(8,128)(2,1)S(1)}, u32[]{:S(2)}, u32[]{:S(2)}) collective-permute-start(bf16[16,32,1024]{2,1,0:T(8,128)(2,1)} %all-to-all-done.1.own.x_2.z_2.own_2), channel_id=1, source_target_pairs={{0,1},{1,0},{2,3},{3,2},{4,5},{5,4},{6,7},{7,6},{8,9},{9,8},{10,11... | collective-permute-start | bytes 3145736 | tf_op jit(solution)/shard_map/ppermute | solution.py:29
  103.6 30.7 %all-to-all-start.2 = ((bf16[16,32,1024]{2,1,0:T(8,128)(2,1)}), bf16[16,32,1024]{2,1,0:T(8,128)(2,1)S(1)}, u32[]{:S(2)}, u32[]{:S(2)}) async-start(bf16[16,32,1024]{2,1,0:T(8,128)(2,1)} %bitcast.30), calls=%async_computation.2 | async-start | bytes 2097152 | tf_op jit(solution)/shard_map/all_to_all | solution.py:75
  111.4 1.0 copy-start.4
  121.1 2.2 %collective-permute-start.10 = (bf16[256,1024]{1,0:T(8,128)(2,1)}, bf16[256,1024]{1,0:T(8,128)(2,1)S(1)}, u32[]{:S(2)}, u32[]{:S(2)}) collective-permute-start(bf16[256,1024]{1,0:T(8,128)(2,1)} %get-tuple-element.56), channel_id=1, source_target_pairs={{0,1},{1,0},{2,3},{3,2},{4,5},{5,4},{6,7},{7,6},{8,9},{9,8},{10,11... | collective-permute-start | bytes 1572872 | tf_op jit(solution)/shard_map/ppermute | solution.py:29
  134.4 32.0 %all-to-all-start.3 = ((bf16[16,16,1024]{2,1,0:T(8,128)(2,1)}), bf16[16,16,1024]{2,1,0:T(8,128)(2,1)S(1)}, u32[]{:S(2)}, u32[]{:S(2)}) async-start(bf16[16,16,1024]{2,1,0:T(8,128)(2,1)} %bitcast.32), calls=%async_computation.3 | async-start | bytes 1048576 | tf_op jit(solution)/shard_map/all_to_all | solution.py:75
  144.4 1.5 collective-permute-start.12
  146.7 9.4 %collective-permute-start.15 = (f32[16,1024]{1,0:T(8,128)S(1)}, f32[16,1024]{1,0:T(8,128)S(1)}, u32[]{:S(2)}, u32[]{:S(2)}) collective-permute-start(f32[16,1024]{1,0:T(8,128)S(1)} %add.155), channel_id=1, source_target_pairs={{0,6},{2,4},{4,2},{6,0},{8,14},{10,12},{12,10},{14,8},{16,22},{18,... | collective-permute-start | bytes 196616 | tf_op jit(solution)/shard_map/ppermute | solution.py:233
  149.6 6.5 %collective-permute-start.14 = (f32[16,1024]{1,0:T(8,128)S(1)}, f32[16,1024]{1,0:T(8,128)S(1)}, u32[]{:S(2)}, u32[]{:S(2)}) collective-permute-start(f32[16,1024]{1,0:T(8,128)S(1)} %add.155), channel_id=1, source_target_pairs={{0,4},{2,6},{4,0},{6,2},{8,12},{10,14},{12,8},{14,10},{16,20},{18,... | collective-permute-start | bytes 196616 | tf_op jit(solution)/shard_map/ppermute | solution.py:233
  150.1 5.9 %collective-permute-start.13 = (f32[16,1024]{1,0:T(8,128)S(1)}, f32[16,1024]{1,0:T(8,128)S(1)}, u32[]{:S(2)}, u32[]{:S(2)}) collective-permute-start(f32[16,1024]{1,0:T(8,128)S(1)} %add.155), channel_id=1, source_target_pairs={{0,2},{2,0},{4,6},{6,4},{8,10},{10,8},{12,14},{14,12},{16,18},{18,... | collective-permute-start | bytes 196616 | tf_op jit(solution)/shard_map/ppermute | solution.py:233
  156.1 7.8 %collective-permute-start.16 = (f32[16,1024]{1,0:T(8,128)S(1)}, f32[16,1024]{1,0:T(8,128)S(1)}, u32[]{:S(2)}, u32[]{:S(2)}) collective-permute-start(f32[16,1024]{1,0:T(8,128)S(1)} %add_add_fusion.1), channel_id=1, source_target_pairs={{0,8},{2,10},{4,12},{6,14},{8,0},{10,2},{12,4},{14,6},{16,24},{18,... | collective-permute-start | bytes 196616 | tf_op jit(solution)/shard_map/ppermute | solution.py:233
  158.1 8.7 %copy-start.6 = (bf16[256,1024]{1,0:T(8,128)(2,1)S(1)}, bf16[256,1024]{1,0:T(8,128)(2,1)}, u32[]{:S(2)}) copy-start(bf16[256,1024]{1,0:T(8,128)(2,1)} %latents.1) | copy-start | bytes 1572868
  163.9 5.5 %collective-permute-start.17 = (f32[16,1024]{1,0:T(8,128)S(1)}, f32[16,1024]{1,0:T(8,128)S(1)}, u32[]{:S(2)}, u32[]{:S(2)}) collective-permute-start(f32[16,1024]{1,0:T(8,128)S(1)} %add.159), channel_id=1, source_target_pairs={{0,16},{2,18},{4,20},{6,22},{8,24},{10,26},{12,28},{14,30},{16,0},... | collective-permute-start | bytes 196616 | tf_op jit(solution)/shard_map/ppermute | solution.py:233
  166.7 3.3 %copy-start.7 = (bf16[256,1024]{1,0:T(8,128)(2,1)S(1)}, bf16[256,1024]{1,0:T(8,128)(2,1)}, u32[]{:S(2)}) copy-start(bf16[256,1024]{1,0:T(8,128)(2,1)} %cotangent.1) | copy-start | bytes 1572868
  167.4 2.6 %collective-permute-start.11 = (f32[2,256]{1,0:T(2,128)S(1)}, f32[2,256]{1,0:T(2,128)S(1)}, u32[]{:S(2)}, u32[]{:S(2)}) collective-permute-start(f32[2,256]{1,0:T(2,128)S(1)} %pad_maximum_fusion.7), channel_id=1, source_target_pairs={{0,1},{1,0},{2,3},{3,2},{4,5},{5,4},{6,7},{7,6},{8,9},{9,8},{10,11... | collective-permute-start | bytes 6152 | tf_op jit(solution)/shard_map/ppermute | solution.py:29
